TPU v7x, 512 devices: a whole 4x4x16 slice. The times are simulated.
512 devices in a mesh: gx: 16 (over z_hi, y, core), gy: 4 (over x), gz: 8 (over z_lo).
Axes of the slice: x: 4, y: 4, z: 16 (z_hi: 2, z_lo: 8; z = z_hi * 8 + z_lo), core: 2. Of those that a mesh axis runs over, the one named last changes fastest.
Arguments:
- body_load: float32 [32, 16, 64, 192], P('gx', 'gy', 'gz'), may hold values from -6 to 6
- probe_load: float32 [32, 16, 64, 192], P('gx', 'gy', 'gz'), may hold values from -6 to 6
- density: float32 [32, 16, 64], P('gx', 'gy', 'gz'), may hold values from 0.3 to 1
- link_types: int32 [32, 16, 64, 7], P('gx', 'gy', 'gz'), may hold values from 0 to 4, as said below
- off_blocks: bfloat16 [4, 192, 192], replicated, may hold values from -0.4375 to 0.4375
- self_blocks: bfloat16 [4, 192, 192], replicated, as said below
- block_owner: int32 [32, 16, 64], P('gx', 'gy', 'gz'), may hold values from 0 to 4095, as said below
Outputs:
- state_field: float32 [32, 16, 64, 192], P('gx', 'gy', 'gz')
- adjoint_field: float32 [32, 16, 64, 192], P('gx', 'gy', 'gz')
- coarse_sensitivity: float32 [4096], P(('gx', 'gy', 'gz'))
Inputs may be any that keep to these rules, and one draw needn't show every extreme that they name: `link_types`: entries 0, 1, 2 of a group name the kind of its coupling to the next group along the first, second and third dimension (4: no coupling, always so on the grid's last layer); entry 3 + k equals entry k of the group one step lower along dimension k (4 on the first layer); entry 6 names the kind of the group's own block and is below 4. `block_owner`: every design block is named by exactly 8 node groups. `self_blocks`: each own block is symmetric and its diagonal entries exceed 3.8.
All inputs are finite; a program needn't handle non-finite values.
Results may differ from a plain program's by a relative error of at most 0.0012.
Values may be sent and summed in bfloat16 or wider, within the bound.
A program may use at most 64 MiB of HBM per device.

v0:
```python
import jax
import jax.numpy as jnp
from jax import lax
from jax.sharding import PartitionSpec as P

ITERS = 4
GPB = 8


def with_halo(array, sides, width):
    for axis, dim in sides:
        peers, length = (lax.axis_size(axis), array.shape[dim])
        up = [(i, (i + 1) % peers) for i in range(peers - 1)]
        down = [(j, i) for i, j in up]
        last = lax.slice_in_dim(array, length - width, length, axis=dim)
        initial = lax.slice_in_dim(array, 0, width, axis=dim)
        before = lax.ppermute(last, axis, up)
        after = lax.ppermute(initial, axis, down)
        array = jnp.concatenate([before, array, after], axis=dim)
    return array


def level_masks(type_codes, level_count):
    levels = lax.broadcasted_iota(jnp.int32, type_codes.shape + (level_count,), 3)
    return (type_codes[..., None] == levels).astype(jnp.bfloat16)


def typed_product(window, selector, block_table):
    spread = window[:, :, :, :, None, :] * selector[None, :, :, :, :, None]
    flattened = spread.reshape(-1, block_table.shape[0])
    return jnp.dot(flattened, block_table, preferred_element_type=jnp.float32).reshape(window.shape)


def cut_window(padded, shift):
    span_x = padded.shape[1] - 2
    span_y = padded.shape[2] - 2
    span_z = padded.shape[3] - 2
    return padded[
        :,
        1 + shift[0] : 1 + shift[0] + span_x,
        1 + shift[1] : 1 + shift[1] + span_y,
        1 + shift[2] : 1 + shift[2] + span_z,
        :,
    ]


def local_image(padded, selectors, tables, stiff_scale):
    up_table, low_table, own_table = tables
    accumulated = typed_product(cut_window(padded, (0, 0, 0)), selectors[6], own_table)
    offsets = ((1, 0, 0), (0, 1, 0), (0, 0, 1))
    for k in range(3):
        upper = offsets[k]
        lower = (-upper[0], -upper[1], -upper[2])
        accumulated = accumulated + typed_product(cut_window(padded, upper), selectors[k], up_table)
        accumulated = accumulated + typed_product(
            cut_window(padded, lower), selectors[3 + k], low_table
        )
    return accumulated * stiff_scale[None, :, :, :, None]


def local(body_load, probe_load, density, link_types, off_blocks, self_blocks, block_owner):
    dof_count = body_load.shape[-1]
    type_count = off_blocks.shape[0]
    self_count = self_blocks.shape[0]
    stiff_scale = density**1.5
    selectors = [level_masks(link_types[..., j], type_count) for j in range(6)]
    selectors.append(level_masks(link_types[..., 6], self_count))
    up_table = jnp.swapaxes(off_blocks, 1, 2).reshape(type_count * dof_count, dof_count)
    low_table = off_blocks.reshape(type_count * dof_count, dof_count)
    own_table = self_blocks.reshape(self_count * dof_count, dof_count)
    tables = (up_table, low_table, own_table)
    diagonals = jnp.diagonal(self_blocks, axis1=1, axis2=2).astype(jnp.float32)
    pivots = jnp.zeros(body_load.shape, jnp.float32)
    for level in range(self_count):
        pivots = (
            pivots + selectors[6][..., level : level + 1].astype(jnp.float32) * diagonals[level]
        )
    targets = jnp.stack([body_load, probe_load])
    residual = targets
    solution = jnp.zeros_like(targets)
    for sweep in range(ITERS):
        precond = residual / pivots[None]
        shipped = (precond * stiff_scale[None, :, :, :, None]).astype(jnp.bfloat16)
        padded = with_halo(shipped, (("gx", 1), ("gy", 2), ("gz", 3)), 1)
        image_field = local_image(padded, selectors, tables, stiff_scale)
        projected = jnp.sum(residual * image_field, axis=(1, 2, 3, 4))
        energy = jnp.sum(image_field * image_field, axis=(1, 2, 3, 4))
        projected, energy = lax.psum((projected, energy), ("gx", "gy", "gz"))
        step_size = projected / (energy + 1e-06)
        solution = solution + step_size[:, None, None, None, None] * precond
        residual = residual - step_size[:, None, None, None, None] * image_field
    applied = targets - residual
    bracket = jnp.sum(solution[1] * applied[0] + solution[0] * applied[1], axis=-1)
    sensitivity = -1.5 * bracket / density
    weighted = density * sensitivity
    groups_here = density.shape[0] * density.shape[1] * density.shape[2]
    blocks_here = groups_here // GPB
    size_x = lax.axis_size("gx")
    size_y = lax.axis_size("gy")
    size_z = lax.axis_size("gz")
    block_total = blocks_here * size_x * size_y * size_z
    owners = block_owner.reshape(-1)
    numerator = jnp.zeros((block_total,), jnp.float32).at[owners].add(weighted.reshape(-1))
    denominator = jnp.zeros((block_total,), jnp.float32).at[owners].add(density.reshape(-1))
    numerator, denominator = (
        lax.psum_scatter(numerator, ("gx", "gy", "gz"), scatter_dimension=0, tiled=True),
        lax.psum_scatter(denominator, ("gx", "gy", "gz"), scatter_dimension=0, tiled=True),
    )
    return (solution[0], solution[1], numerator / denominator)


def solution(mesh):
    in_specs = (
        P("gx", "gy", "gz", None),
        P("gx", "gy", "gz", None),
        P("gx", "gy", "gz"),
        P("gx", "gy", "gz", None),
        P(),
        P(),
        P("gx", "gy", "gz"),
    )
    out_specs = (P("gx", "gy", "gz", None), P("gx", "gy", "gz", None), P(("gx", "gy", "gz")))
    return jax.shard_map(local, mesh=mesh, in_specs=in_specs, out_specs=out_specs, check_vma=False)
```

profile of v0, /device:TPU:1, one launch (start us, length us, event | category | flops | bytes accessed | tf_op | source)
XLA Modules:
  0.0 689.2 jit_solution(9838900810073035173)
XLA Ops:
  1.5 7.8 %copy.38 = bf16[4,192,192]{0,2,1:T(8,128)(2,1)} copy(bf16[4,192,192]{2,1,0:T(8,128)(2,1)} %param.12) | data formatting | bytes 589824 | tf_op args[5]
  9.3 5.3 gather_fusion
  15.2 8.8 %collective-permute-start = (bf16[2,1,4,8,192]{4,3,2,1,0:T(8,128)(2,1)S(1)}, bf16[2,1,4,8,192]{4,3,2,1,0:T(8,128)(2,1)S(1)}, u32[]{:S(2)}, u32[]{:S(2)}) collective-permute-start(bf16[2,1,4,8,192]{4,3,2,1,0:T(8,128)(2,1)S(1)} %get-tuple-element.83), channel_id=1, source_target_pairs={{32,0},{64,32},{96,64},{128,96},{160,128},{192,160},{224,192},{256... | collective-permute-start | bytes 73736 | tf_op jit(solution)/shard_map/ppermute | solution.py:18
  24.0 1.9 collective-permute-start.1
  27.2 1.3 collective-permute-start.2
  28.5 4.0 collective-permute-start.3
  33.5 1.3 collective-permute-start.4
  34.8 4.0 collective-permute-start.5
  41.4 125.0 %all-reduce.6 = (f32[2]{0:T(128)S(1)}, f32[2]{0:T(128)S(1)}) all-reduce(f32[2]{0:T(128)S(1)} %get-tuple-element.10, f32[2]{0:T(128)S(1)} %get-tuple-element.9), channel_id=1, replica_groups=mesh['gx'=16,'gy'=4,'gz'=8] {'gx','gy','gz'}, use_global_device_ids=true, to_apply=%region_1.2 | all-reduce | flops 4 | bytes 32 | tf_op jit(solution)/shard_map/psum | solution.py:88
  166.6 2.9 collective-permute-start.6
  169.5 2.7 collective-permute-start.7
  173.2 1.3 collective-permute-start.8
  174.5 4.0 collective-permute-start.9
  179.6 1.3 collective-permute-start.10
  180.9 4.0 collective-permute-start.11
  187.5 117.6 %all-reduce.5 = (f32[2]{0:T(128)S(1)}, f32[2]{0:T(128)S(1)}) all-reduce(f32[2]{0:T(128)S(1)} %get-tuple-element.8, f32[2]{0:T(128)S(1)} %get-tuple-element.7), channel_id=1, replica_groups=mesh['gx'=16,'gy'=4,'gz'=8] {'gx','gy','gz'}, use_global_device_ids=true, to_apply=%region_5.6 | all-reduce | flops 4 | bytes 32 | tf_op jit(solution)/shard_map/psum | solution.py:88
  305.2 2.6 collective-permute-start.12
  307.8 3.0 collective-permute-start.13
  311.8 1.3 collective-permute-start.14
  313.1 4.0 collective-permute-start.15
  318.3 1.3 collective-permute-start.16
  319.6 4.0 collective-permute-start.17
  326.2 120.1 %all-reduce.4 = (f32[2]{0:T(128)S(1)}, f32[2]{0:T(128)S(1)}) all-reduce(f32[2]{0:T(128)S(1)} %get-tuple-element.6, f32[2]{0:T(128)S(1)} %get-tuple-element.5), channel_id=1, replica_groups=mesh['gx'=16,'gy'=4,'gz'=8] {'gx','gy','gz'}, use_global_device_ids=true, to_apply=%region_9.10 | all-reduce | flops 4 | bytes 32 | tf_op jit(solution)/shard_map/psum | solution.py:88
  446.4 3.1 collective-permute-start.18
  449.6 2.5 collective-permute-start.19
  452.1 1.1 scatter_custom_fusion.1
  453.3 1.3 collective-permute-start.20
  454.6 4.0 collective-permute-start.21
  459.7 1.3 collective-permute-start.22
  461.0 4.0 collective-permute-start.23
  467.6 118.0 %all-reduce.3 = (f32[2]{0:T(128)S(1)}, f32[2]{0:T(128)S(1)}) all-reduce(f32[2]{0:T(128)S(1)} %get-tuple-element.4, f32[2]{0:T(128)S(1)} %get-tuple-element.3), channel_id=1, replica_groups=mesh['gx'=16,'gy'=4,'gz'=8] {'gx','gy','gz'}, use_global_device_ids=true, to_apply=%region_13.14 | all-reduce | flops 4 | bytes 32 | tf_op jit(solution)/shard_map/psum | solution.py:88
  587.4 101.2 %all-reduce.2 = (f32[4096]{0:T(1024)S(1)}, f32[4096]{0:T(1024)S(1)}) all-reduce(f32[4096]{0:T(1024)S(1)} %scatter_custom_fusion.1, f32[4096]{0:T(1024)S(1)} %scatter_custom_fusion), channel_id=3, replica_groups=mesh['gx'=16,'gy'=4,'gz'=8] {'gx','gy','gz'}, use_global_device_ids=true, to_apply=%region_20.21.clone | all-reduce | flops 8192 | bytes 65536
  (115 shorter events, 21.9 us)
Async XLA Ops:
  0.6 38.2 %copy-start = (bf16[4,192,192]{2,1,0:T(8,128)(2,1)S(1)}, bf16[4,192,192]{2,1,0:T(8,128)(2,1)}, u32[]{:S(2)}) copy-start(bf16[4,192,192]{2,1,0:T(8,128)(2,1)} %param.11) | copy-start | bytes 884740
  0.6 31.8 %copy-start.3 = (bf16[4,192,192]{2,1,0:T(8,128)(2,1)S(1)}, bf16[4,192,192]{2,1,0:T(8,128)(2,1)}, u32[]{:S(2)}) copy-start(bf16[4,192,192]{2,1,0:T(8,128)(2,1)} %param.12) | copy-start | bytes 884740
  0.7 14.3 %copy-start.5 = (s32[2,4,8,7]{2,1,3,0:T(4,128)S(1)}, s32[2,4,8,7]{2,1,3,0:T(4,128)}, u32[]{:S(2)}) copy-start(s32[2,4,8,7]{2,1,3,0:T(4,128)} %param.10) | copy-start | bytes 5380
  0.7 14.5 %copy-start.1 = (f32[2,4,8,192]{3,2,1,0:T(8,128)S(1)}, f32[2,4,8,192]{3,2,1,0:T(8,128)}, u32[]{:S(2)}) copy-start(f32[2,4,8,192]{3,2,1,0:T(8,128)} %param.8) | copy-start | bytes 147460
  0.7 14.5 %copy-start.2 = (f32[2,4,8,192]{3,2,1,0:T(8,128)S(1)}, f32[2,4,8,192]{3,2,1,0:T(8,128)}, u32[]{:S(2)}) copy-start(f32[2,4,8,192]{3,2,1,0:T(8,128)} %param.7) | copy-start | bytes 147460
  15.2 10.8 %collective-permute-start = (bf16[2,1,4,8,192]{4,3,2,1,0:T(8,128)(2,1)S(1)}, bf16[2,1,4,8,192]{4,3,2,1,0:T(8,128)(2,1)S(1)}, u32[]{:S(2)}, u32[]{:S(2)}) collective-permute-start(bf16[2,1,4,8,192]{4,3,2,1,0:T(8,128)(2,1)S(1)} %get-tuple-element.83), channel_id=1, source_target_pairs={{32,0},{64,32},{96,64},{128,96},{160,128},{192,160},{224,192},{256... | collective-permute-start | bytes 73736 | tf_op jit(solution)/shard_map/ppermute | solution.py:18
  24.0 3.1 collective-permute-start.1
  27.2 5.6 collective-permute-start.2
  28.5 5.0 collective-permute-start.3
  33.5 6.0 collective-permute-start.4
  34.8 5.2 collective-permute-start.5
  39.2 271.5 %copy-start.6 = (s32[2,4,8]{2,1,0:T(4,128)S(1)}, s32[2,4,8]{2,1,0:T(4,128)}, u32[]{:S(2)}) copy-start(s32[2,4,8]{2,1,0:T(4,128)} %param.13) | copy-start | bytes 772
  166.6 5.6 collective-permute-start.6
  169.5 3.7 collective-permute-start.7
  173.2 5.6 collective-permute-start.8
  174.5 5.0 collective-permute-start.9
  179.6 6.0 collective-permute-start.10
  180.9 5.2 collective-permute-start.11
  184.9 267.1 %copy-start.4 = (f32[2,4,8]{2,1,0:T(4,128)S(1)}, f32[2,4,8]{2,1,0:T(4,128)}, u32[]{:S(2)}) copy-start(f32[2,4,8]{2,1,0:T(4,128)} %param.9) | copy-start | bytes 772
  305.2 5.7 collective-permute-start.12
  307.8 4.0 collective-permute-start.13
  311.8 5.6 collective-permute-start.14
  313.1 5.2 collective-permute-start.15
  318.3 6.0 collective-permute-start.16
  319.6 5.2 collective-permute-start.17
  446.4 6.8 collective-permute-start.18
  449.6 3.7 collective-permute-start.19
  453.3 5.6 collective-permute-start.20
  454.6 5.0 collective-permute-start.21
  459.7 6.0 collective-permute-start.22
  461.0 5.2 collective-permute-start.23
where the time goes:
time: 691 us; the launch traced here: 689 us
  blocking collectives  582 us (84%)
  starting transfers between devices  69.6 us (10%)
  local copies, waits for them, and re-layouts  14.6 us (2%)
  matrix products  9.27 us (1%)
  waiting for transfers between devices  7.56 us (1%)
    psum x4, blocking collectives, local(): projected, energy = lax.psum((projected, energy), ('gx', 'gy', 'gz'))  481 us
    unnamed x1, blocking collectives  101 us
    ppermute x12, starting transfers between devices, with_halo(): before = lax.ppermute(last, axis, up)  41.9 us
    ppermute x12, starting transfers between devices, with_halo(): after = lax.ppermute(initial, axis, down)  27.7 us
  transfers between devices with their start and end apart: 24, of which 11 were waited for; matrix products, arithmetic and copies ran while one was open for 1% of the time, Pallas kernels for 0%

commit v1 on v0

v1 whole, which is shorter than its diff:
```python
import functools

import jax
import jax.numpy as jnp
from jax import lax
from jax.experimental import pallas as pl
from jax.experimental.pallas import tpu as pltpu
from jax.sharding import PartitionSpec as P

MESH = pl.DeviceIdType.MESH
F32, BF16 = jnp.float32, jnp.bfloat16
ITERS = 4
GPB = 8
NX, NY, NZ = 2, 4, 8
G = NX * NY * NZ
DOF, LANES = 192, 256
UPX, LOWX, LOWY, UPY, LOWZ, UPZ, ROWS = 64, 96, 128, 144, 160, 176, 192
SX, SY, SZ, CY = 16, 4, 8, 8
PLANE, ZLINE = 32, 16
LOCAL_GAIN = (3 / 2.125) ** 0.5
NT_DIMS = (((1,), (1,)), ((), ()))


def iota(shape, dim):
    return lax.broadcasted_iota(jnp.int32, shape, dim)


def total(values):
    values = list(values)
    while len(values) > 1:
        pairs = [values[i] + values[i + 1] for i in range(0, len(values) - 1, 2)]
        values = pairs + values[len(pairs) * 2 :]
    return values[0]


def place(i, j):
    i, j = min(i, j), max(i, j)
    return i * 5 - i * (i - 1) // 2 + (j - i)


def entries(row, size):
    lane = iota(row.shape, 1)
    table = {}
    for i in range(size):
        for j in range(i, size):
            table[i, j] = table[j, i] = jnp.sum(
                jnp.where(lane == place(i, j), row, 0.0), axis=1, keepdims=True
            )
    return table


def bilinear(left, table, right):
    return total(
        left[i] * total(table[i, j] * right[j] for j in right) for i in left
    )


def sweeps(table, count, image):
    one = jnp.ones_like(table[0, 0])
    residual, answer, steps = {0: one}, {}, []
    for _ in range(count):
        moved = image(residual)
        projected = bilinear(residual, table, moved)
        energy = bilinear(moved, table, moved)
        step = projected / (energy + 1e-6)
        steps.append(step)
        for i, c in residual.items():
            answer[i] = answer[i] + step * c if i in answer else step * c
        for i, c in moved.items():
            residual[i] = residual[i] - step * c if i in residual else -(step * c)
    return steps, answer, residual


def kernel(body, probe, dens, links, offb, selfb, owner, state_out, adjoint_out, coarse_out,
           x_first, x_rest, faces_first, faces_rest, pick, table, v, su, sc, rp, hot, rr, mp, mps, mz, mzs,
           hs, hr, ps, pr, zs, zr):
    gx, gy, gz = lax.axis_index("gx"), lax.axis_index("gy"), lax.axis_index("gz")
    zh, yc = gx // CY, gx % CY
    me_p = yc * SY + gy
    me_z = zh * SZ + gz
    far = jnp.logical_or(gx == CY - 1, gx == CY)

    def plane_peer(i):
        p = (me_p + 1 + i) % PLANE
        return (zh * CY + p // SY, p % SY, gz)

    def line_peer(i):
        q = (me_z + 1 + i) % ZLINE
        return (q // SZ * CY + yc, gy, q % SZ)

    barrier = pltpu.get_barrier_semaphore()

    def greet_plane(i, _):
        pl.semaphore_signal(barrier, inc=1, device_id=plane_peer(i), device_id_type=MESH)
        return 0

    def greet_line(i, _):
        pl.semaphore_signal(barrier, inc=1, device_id=line_peer(i), device_id_type=MESH)
        return 0

    lax.fori_loop(0, ZLINE - 1, greet_line, 0)

    @pl.when(far)
    def _():
        pl.semaphore_signal(
            barrier, inc=1, device_id=(2 * CY - 1 - gx, gy, gz), device_id_type=MESH
        )

    lax.fori_loop(0, PLANE - 1, greet_plane, 0)

    sends = (
        (gx < SX - 1, (gx + 1, gy, gz)),
        (gx > 0, (gx - 1, gy, gz)),
        (gy < SY - 1, (gx, gy + 1, gz)),
        (gy > 0, (gx, gy - 1, gz)),
        (gz < SZ - 1, (gx, gy, gz + 1)),
        (gz > 0, (gx, gy, gz - 1)),
    )
    lands = ((LOWX, 32), (UPX, 32), (LOWY, 16), (UPY, 16), (LOWZ, 16), (UPZ, 16))
    comes = tuple(sends[d ^ 1][0] for d in range(6))

    def halo(k, d):
        at, size = lands[d]
        x, faces = (x_first, faces_first) if k == 0 else (x_rest.at[k - 1], faces_rest.at[k - 1])
        if d < 2:
            src = x.at[pl.ds(32 - 32 * d, 32)]
        else:
            src = faces.at[pl.ds(16 * (d - 2), 16)]
        return pltpu.make_async_remote_copy(
            src_ref=src,
            dst_ref=x.at[pl.ds(at, size)],
            send_sem=hs.at[k, d],
            recv_sem=hr.at[k, d],
            device_id=sends[d][1],
            device_id_type=MESH,
        )

    def start_halos(k):
        for d in range(6):
            @pl.when(sends[d][0])
            def _():
                halo(k, d).start()

    def wait_halos(k):
        for d in range(6):
            @pl.when(comes[d])
            def _():
                halo(k, d).wait_recv()

    for d in range(6):
        at, size = lands[d]

        @pl.when(jnp.logical_not(comes[d]))
        def _():
            x_first[pl.ds(at, size), :] = jnp.zeros((size, 2 * LANES), BF16)
            x_rest[:, pl.ds(at, size), :] = jnp.zeros((ITERS - 1, size, 4 * LANES), BF16)

    eye8 = iota((8, 8), 0) == iota((8, 8), 1)

    def column(row_of):
        return jnp.concatenate(
            [
                jnp.sum(
                    jnp.where(eye8, jnp.broadcast_to(row_of(a, b).astype(F32), (8, 8)), 0.0),
                    axis=1,
                    keepdims=True,
                )
                for a in range(NX)
                for b in range(NY)
            ],
            axis=0,
        )

    kinds = [column(lambda a, b: links[a, k, b : b + 1, :]) for k in range(7)]
    density = column(lambda a, b: dens[a, b : b + 1, :])
    owners = column(lambda a, b: owner[a, b : b + 1, :])

    scale = density * jnp.sqrt(density)
    eye = iota((DOF, DOF), 0) == iota((DOF, DOF), 1)
    eye_low = jnp.where(eye, 1.0, 0.0).astype(BF16)
    pivots = jnp.zeros((G, DOF), F32)
    table[...] = jnp.zeros(table.shape, BF16)
    for t in range(4):
        block = selfb[t]
        diagonal = jnp.sum(jnp.where(eye, block.astype(F32), 0.0), axis=0, keepdims=True)
        pivots = jnp.where(kinds[6] == float(t), diagonal, pivots)
        upper = lax.dot_general(eye_low, offb[t], NT_DIMS, preferred_element_type=F32)
        table[pl.ds(t * LANES, DOF), pl.ds(0, DOF)] = upper.astype(BF16)
        table[pl.ds((4 + t) * LANES, DOF), pl.ds(0, DOF)] = offb[t]
        table[pl.ds((8 + t) * LANES, DOF), pl.ds(0, DOF)] = block
    rp[...] = jnp.ones((G, LANES), F32)
    rp[:, pl.ds(0, DOF)] = 1.0 / pivots
    sc[...] = jnp.broadcast_to(scale, (G, LANES))
    su[...] = rp[...] * sc[...]

    v[0] = jnp.zeros((2 * G, LANES), F32)
    v[0, pl.ds(0, G), pl.ds(0, DOF)] = body[...].reshape(G, DOF)
    v[0, pl.ds(G, G), pl.ds(0, DOF)] = probe[...].reshape(G, DOF)

    g = iota((G, 1), 0)
    gl, gyy, gzz = g // 32, g // 8 % 4, g % 8
    sources = (
        jnp.where(gl == 0, g + 32, UPX + g - 32),
        jnp.where(gyy < NY - 1, g + 8, UPY + gl * 8 + gzz),
        jnp.where(gzz < NZ - 1, g + 1, UPZ + gl * 4 + gyy),
        jnp.where(gl == 0, LOWX + g, g - 32),
        jnp.where(gyy > 0, g - 8, LOWY + gl * 8 + gzz),
        jnp.where(gzz > 0, g - 1, LOWZ + gl * 4 + gyy),
    )
    across = iota((G, ROWS), 1).astype(F32)
    sources = [s.astype(F32) for s in sources]
    for side in range(2):
        for t in range(4):
            chosen = jnp.zeros((G, ROWS), F32)
            for k in range(3 * side, 3 * side + 3):
                code = jnp.where(kinds[k] == float(t), sources[k], -1.0)
                chosen = jnp.where(across == code, 1.0, chosen)
            pick[pl.ds((4 * side + t) * G, G), :] = chosen.astype(BF16)
    for t in range(4):
        code = jnp.where(kinds[6] == float(t), g.astype(F32), -1.0)
        pick[pl.ds((8 + t) * G, G), :] = jnp.where(across == code, 1.0, 0.0).astype(BF16)

    r = iota((G, 1), 0)
    r16 = r % 16
    face_y = r16 // 8 * 32 + r16 % 8
    face_z = jnp.where(r16 < 8, r16 // 4 * 32 + r16 % 4 * 8, -64)
    face = jnp.where(
        r < 16, face_y + 24, jnp.where(r < 32, face_y, jnp.where(r < 48, face_z + 7, face_z))
    )
    outer = jnp.where(iota((G, G), 1) == face, 1.0, 0.0).astype(BF16)

    def both(a):
        return jnp.concatenate([a, a], axis=0)

    def scaled(field, parts):
        u = field * both(su[...])
        high = u.astype(BF16)
        out = [high[:G], high[G:]]
        if parts == 2:
            low = (u - high.astype(F32)).astype(BF16)
            out += [low[:G], low[G:]]
        return jnp.concatenate(out, axis=1)

    def wide(a, count):
        return [
            jnp.concatenate(
                [a[t * G : (t + 1) * G, f * LANES : (f + 1) * LANES] for t in range(count)],
                axis=1,
            )
            for f in range(a.shape[1] // LANES)
        ]

    def fold(a):
        return a[: 2 * G] + a[2 * G :] if a.shape[0] == 4 * G else a

    def image(sent, width, gain):
        z = jnp.dot(pick[:, pl.ds(0, width)], sent, preferred_element_type=F32)
        off, own = z[: 8 * G], z[8 * G :].astype(BF16)
        if off.shape[1] == 4 * LANES:
            off = off[:, : 2 * LANES] + off[:, 2 * LANES :]
        high = off.astype(BF16)
        low = (off - high.astype(F32)).astype(BF16)
        left = jnp.concatenate(wide(high, 8) + wide(low, 8), axis=0)
        a = jnp.dot(left, table[pl.ds(0, 8 * LANES)], preferred_element_type=F32)
        b = jnp.dot(
            jnp.concatenate(wide(own, 4), axis=0),
            table[pl.ds(8 * LANES, 4 * LANES)],
            preferred_element_type=F32,
        )
        a = fold(a)
        if gain != 1.0:
            a = a * gain
        return (a + fold(b)) * both(sc[...])

    def ship(k, field):
        sent = scaled(field, 1 if k == 0 else 2)
        outside = jnp.dot(outer, sent, preferred_element_type=F32).astype(BF16)
        if k == 0:
            x_first[pl.ds(0, G), :] = sent
            faces_first[...] = outside
        else:
            x_rest[k - 1, pl.ds(0, G), :] = sent
            faces_rest[k - 1] = outside

    def gram(fields, i, j):
        product = fields[i] * fields[j]
        for f in range(2):
            part = jnp.sum(product[f * G : (f + 1) * G], axis=0, keepdims=True)
            rr[pl.ds(f * 16 + place(i, j), 1), :] = part[:, :128] + part[:, 128:]

    def gram_rows():
        sums = jnp.sum(rr[...], axis=1, keepdims=True)
        spot = iota((16, 128), 0) == iota((16, 128), 1)
        return [
            jnp.sum(jnp.where(spot, sums[f * 16 : f * 16 + 16], 0.0), axis=0, keepdims=True)
            for f in range(2)
        ]

    def start_plane(e):
        def one(i, _):
            pltpu.make_async_remote_copy(
                src_ref=mp.at[e], dst_ref=mps.at[e, PLANE - 2 - i],
                send_sem=ps.at[e], recv_sem=pr.at[e],
                device_id=plane_peer(i), device_id_type=MESH,
            ).start()
            return 0

        lax.fori_loop(0, PLANE - 1, one, 0)

    def start_line(e):
        def one(i, _):
            pltpu.make_async_remote_copy(
                src_ref=mz.at[e], dst_ref=mzs.at[e, ZLINE - 2 - i],
                send_sem=zs.at[e], recv_sem=zr.at[e],
                device_id=line_peer(i), device_id_type=MESH,
            ).start()
            return 0

        lax.fori_loop(0, ZLINE - 1, one, 0)

    def wait_all(buffer, sem):
        pltpu.make_async_copy(buffer, buffer, sem).wait()

    rr[...] = jnp.zeros(rr.shape, F32)
    mp[...] = jnp.zeros(mp.shape, F32)
    mz[...] = jnp.zeros(mz.shape, F32)
    ship(0, v[0])

    inner = [v[0]]
    for _ in range(ITERS - 1):
        inner.append(image(scaled(inner[-1], 1), G, LOCAL_GAIN))
    for i in range(ITERS):
        for j in range(i, ITERS):
            gram(inner, i, j)

    half = G * (me_p % 2)
    spread = iota((G, 128), 1) == iota((G, 128), 0) + half

    def as_row(col):
        return jnp.sum(jnp.where(spread, col, 0.0), axis=0, keepdims=True)

    rows = gram_rows()
    mp[0, 0:1, :] = rows[0]
    mp[0, 1:2, :] = rows[1]
    mp[0, 2:3, :] = as_row(owners)
    mp[0, 3:4, :] = as_row(density)

    pl.semaphore_wait(barrier, PLANE - 1 + ZLINE - 1 + far.astype(jnp.int32))
    start_halos(0)
    start_plane(0)
    wait_all(mps.at[0], pr.at[0])
    mz[0] = mp[0] + total(mps[0, i] for i in range(PLANE - 1))
    start_line(0)

    def gathered(e, row):
        parts = [mps[e, i, row : row + 1, :] for i in range(PLANE - 1)]
        parts.append(mp[e, row : row + 1, :])
        return [parts[2 * m] + parts[2 * m + 1] for m in range(PLANE // 2)]

    q = iota((128, 1), 0)
    bins = (((q // 64 * CY + yc) * SY + gy) * SZ + q // 8 % 8) * GPB + q % 8
    bins = bins.astype(F32)
    for m, row in enumerate(gathered(0, 2)):
        hot[:, pl.ds(m * 128, 128)] = jnp.where(row == bins, 1.0, 0.0).astype(BF16)

    def by_block(e, row):
        flat = jnp.concatenate(gathered(e, row), axis=1)
        first = flat.astype(BF16).astype(F32)
        rest = flat - first
        second = rest.astype(BF16).astype(F32)
        third = rest - second
        sub = iota((8, flat.shape[1]), 0)
        split = jnp.where(
            sub == 0, first, jnp.where(sub == 1, second, jnp.where(sub == 2, third, 0.0))
        ).astype(BF16)
        sums = lax.dot_general(split, hot[...], NT_DIMS, preferred_element_type=F32)
        return jnp.sum(sums, axis=0, keepdims=True)

    mz[1, 2:3, :] = by_block(0, 3)

    guess = None
    for k in range(ITERS):
        wait_halos(k)
        moved = image(x_first[...] if k == 0 else x_rest[k - 1], ROWS, 1.0)
        if k == 0:
            wait_all(mzs.at[0], zr.at[0])
            row = mz[0, 0:2, :] + total(mzs[0, i, 0:2, :] for i in range(ZLINE - 1))
            guess, _, _ = sweeps(
                entries(row, ITERS), ITERS - 1, lambda c: {i + 1: e for i, e in c.items()}
            )
            guess = [jnp.where((s > 1e-3) & (s < 1e6), s, 1.0) for s in guess]
        if k < ITERS - 1:
            step = jnp.concatenate(
                [jnp.broadcast_to(guess[k][f : f + 1], (G, 1)) for f in range(2)], axis=0
            )
            v[k + 1] = v[k] - step * moved
            ship(k + 1, v[k + 1])
            start_halos(k + 1)
        else:
            v[k + 1] = moved
        for i in range(k + 2):
            gram(v, i, k + 1)
        if k == 0:
            gram(v, 0, 0)

    rows = gram_rows()
    mp[1, 0:1, :] = rows[0]
    mp[1, 1:2, :] = rows[1]
    start_plane(1)
    wait_all(mps.at[1], pr.at[1])
    mz[1, 0:2, :] = mp[1, 0:2, :] + total(mps[1, i, 0:2, :] for i in range(PLANE - 1))
    start_line(1)
    wait_all(mzs.at[1], zr.at[1])
    row = mz[1] + total(mzs[1, i] for i in range(ZLINE - 1))
    below = row[2:3, :]

    inverse = [1.0 / s for s in guess]

    def newton(c):
        out = {}
        for i, e in c.items():
            if i < ITERS - 1:
                part = e * inverse[i]
                out[i] = out[i] + part if i in out else part
                out[i + 1] = out[i + 1] - part if i + 1 in out else -part
            else:
                out[i + 1] = e
        return out

    _, answer, left = sweeps(entries(row[0:2, :], ITERS + 1), ITERS, newton)

    def combine(coefficients, f):
        return total(
            c[f : f + 1, :] * v[i, pl.ds(f * G, G), :] for i, c in coefficients.items()
        )

    solved = [combine(answer, f) * rp[...] for f in range(2)]
    state_out[...] = solved[0][:, :DOF].reshape(state_out.shape)
    adjoint_out[...] = solved[1][:, :DOF].reshape(adjoint_out.shape)
    applied = {i: (1.0 - c if i == 0 else -c) for i, c in left.items()}
    applied = [combine(applied, f) for f in range(2)]
    bracket = jnp.sum(solved[1] * applied[0] + solved[0] * applied[1], axis=1, keepdims=True)
    weighted = density * (-1.5 * bracket / density)
    mp[2, 0:1, :] = as_row(weighted)
    start_plane(2)
    wait_all(mps.at[2], pr.at[2])
    mz[2, 0:1, :] = by_block(2, 0)
    start_line(2)
    wait_all(mzs.at[2], zr.at[2])
    above = mz[2, 0:1, :] + total(mzs[2, i, 0:1, :] for i in range(ZLINE - 1))
    ratio = jnp.where(below > 0.0, above / below, 0.0)
    mine = iota((8, 128), 1) == iota((8, 128), 0) + 8 * me_z
    col = jnp.sum(jnp.where(mine, ratio, 0.0), axis=1, keepdims=True)
    coarse_out[...] = jnp.sum(jnp.where(eye8, col, 0.0), axis=0, keepdims=True)

    for k in range(ITERS):
        for d in range(6):
            @pl.when(sends[d][0])
            def _():
                halo(k, d).wait_send()
    for e in range(3):
        wait_all(mps.at[e], ps.at[e])
        wait_all(mzs.at[e], zs.at[e])


def local(body_load, probe_load, density, link_types, off_blocks, self_blocks, block_owner):
    vmem = pl.BlockSpec(memory_space=pltpu.VMEM)
    state, adjoint, coarse = pl.pallas_call(
        kernel,
        out_shape=(
            jax.ShapeDtypeStruct(body_load.shape, F32),
            jax.ShapeDtypeStruct(body_load.shape, F32),
            jax.ShapeDtypeStruct((1, GPB), F32),
        ),
        in_specs=[vmem] * 7,
        out_specs=(vmem,) * 3,
        scratch_shapes=[
            pltpu.VMEM((ROWS, 2 * LANES), BF16),
            pltpu.VMEM((ITERS - 1, ROWS, 4 * LANES), BF16),
            pltpu.VMEM((G, 2 * LANES), BF16),
            pltpu.VMEM((ITERS - 1, G, 4 * LANES), BF16),
            pltpu.VMEM((12 * G, ROWS), BF16),
            pltpu.VMEM((12 * LANES, LANES), BF16),
            pltpu.VMEM((ITERS + 1, 2 * G, LANES), F32),
            pltpu.VMEM((G, LANES), F32),
            pltpu.VMEM((G, LANES), F32),
            pltpu.VMEM((G, LANES), F32),
            pltpu.VMEM((128, PLANE * G), BF16),
            pltpu.VMEM((32, 128), F32),
            pltpu.VMEM((3, 4, 128), F32),
            pltpu.VMEM((3, PLANE - 1, 4, 128), F32),
            pltpu.VMEM((3, 4, 128), F32),
            pltpu.VMEM((3, ZLINE - 1, 4, 128), F32),
            pltpu.SemaphoreType.DMA((ITERS, 6)),
            pltpu.SemaphoreType.DMA((ITERS, 6)),
            pltpu.SemaphoreType.DMA((3,)),
            pltpu.SemaphoreType.DMA((3,)),
            pltpu.SemaphoreType.DMA((3,)),
            pltpu.SemaphoreType.DMA((3,)),
        ],
        compiler_params=pltpu.CompilerParams(
            collective_id=0, has_side_effects=True, vmem_limit_bytes=60 << 20
        ),
        name="sweeps",
    )(
        body_load,
        probe_load,
        density,
        jnp.transpose(link_types, (0, 3, 1, 2)),
        off_blocks,
        self_blocks,
        block_owner,
    )
    return state, adjoint, coarse.reshape(GPB)


def solution(mesh):
    in_specs = (
        P("gx", "gy", "gz", None),
        P("gx", "gy", "gz", None),
        P("gx", "gy", "gz"),
        P("gx", "gy", "gz", None),
        P(),
        P(),
        P("gx", "gy", "gz"),
    )
    out_specs = (P("gx", "gy", "gz", None), P("gx", "gy", "gz", None), P(("gx", "gy", "gz")))
    return jax.shard_map(local, mesh=mesh, in_specs=in_specs, out_specs=out_specs, check_vma=False)
```

time: 691 us -> 91 us (0.13)
  blocking collectives: 582 us -> 0 us
  Pallas kernels: 0 us -> 87.5 us
  starting transfers between devices: 69.6 us -> 0 us
  local copies, waits for them, and re-layouts: 14.6 us -> 2.65 us
  matrix products: 9.27 us -> 0 us
  waiting for transfers between devices: 7.56 us -> 0 us
    psum x4 -> x0, blocking collectives: 481 us -> none  [local(): projected, energy = lax.psum((projected, energy), ('gx', 'gy', 'gz'))]
    unnamed x1 -> x0, blocking collectives: 101 us -> none
    pallas_call x0 -> x1, Pallas kernels: none -> 87.5 us  [local(): pl.pallas_call(kernel, out_shape=(jax.ShapeDtypeStruct(body_load.shape, F...]
    ppermute x24 -> x0, starting transfers between devices: 69.6 us -> none  [the longest x12 41.9 us: with_halo(): before = lax.ppermute(last, axis, up)]
    dot_general x28 -> x0, matrix products: 9.27 us -> none  [typed_product(): jnp.dot(flattened, block_table, preferred_element_type=jnp.float32)]
    ppermute x24 -> x0, waiting for transfers between devices: 7.56 us -> none  [the longest x12 7.53 us: with_halo(): before = lax.ppermute(last, axis, up)]
  transfers between devices with their start and end apart: 24 -> 0, of which waited for: 11 -> 0; matrix products, arithmetic and copies ran while one was open for 1% -> 0% of each run, Pallas kernels for 0% -> 0%
where the time goes in v1:
time: 91 us; the launch traced here: 90.8 us
  Pallas kernels  87.5 us (96%)
  local copies, waits for them, and re-layouts  2.65 us (3%)
    pallas_call x1, Pallas kernels, local(): pl.pallas_call(kernel, out_shape=(jax.ShapeDtypeStruct(body_load.shape, F...  87.5 us
    unnamed x7, local copies, waits for them, and re-layouts  2.65 us

profile of v1, /device:TPU:1, one launch (start us, length us, event | category | flops | bytes accessed | tf_op | source)
XLA Modules:
  0.0 90.8 jit_solution(14592788936517479975)
XLA Ops:
  0.6 87.5 %sweeps.1 = (f32[2,4,8,192]{3,2,1,0:T(8,128)}, f32[2,4,8,192]{3,2,1,0:T(8,128)}, f32[1,8]{1,0:T(1,128)}) custom-call(f32[2,4,8,192]{3,2,1,0:T(8,128)} %body.1, f32[2,4,8,192]{3,2,1,0:T(8,128)} %probe.1, f32[2,4,8]{2,1,0:T(4,128)} %dens.1, s32[2,7,4,8]{3,2,1,0:T(4,128)} %bitcast.2, bf16[4,192,192]{2,1,0:T(8,128)(2,1)} %offb.1, bf16[4,192,192]{2,1,0:T(8,128)(2,1)} %selfb.1, ...), custom_call_target="tpu_custom_call" | custom-call | tf_op jit(solution)/shard_map/sweeps/pallas_call | solution.py:468
  88.1 0.0 copy-start
  88.1 1.5 %copy.13 = f32[2,4,8,192]{3,2,1,0:T(8,128)} copy(f32[2,4,8,192]{3,2,1,0:T(8,128)} %get-tuple-element.12) | data formatting | bytes 98304
  89.6 0.0 copy-done
  89.6 0.0 copy-start.1
  89.6 0.6 copy.14
  90.3 0.0 copy-done.1
  90.3 0.5 copy.15
Async XLA Ops:
  88.1 1.5 %copy-start = (f32[2,4,8,192]{3,2,1,0:T(8,128)S(1)}, f32[2,4,8,192]{3,2,1,0:T(8,128)}, u32[]{:S(2)}) copy-start(f32[2,4,8,192]{3,2,1,0:T(8,128)} %get-tuple-element.13) | copy-start | bytes 147460
  89.6 0.6 copy-start.1

commit v2 on v1

--- a/solution.py
+++ b/solution.py
@@ -14,7 +14,11 @@
 NX, NY, NZ = 2, 4, 8
 G = NX * NY * NZ
 DOF, LANES = 192, 256
-UPX, LOWX, LOWY, UPY, LOWZ, UPZ, ROWS = 64, 96, 128, 144, 160, 176, 192
+LAYER, DEEP = NY * NZ, 3
+ALL = G + DEEP * LAYER
+UPX, LOWX, LOWY, UPY, LOWZ, UPZ, ROWS = 64, 192, 224, 272, 320, 352, 384
+FACES = (0, 48, 96, 128)
+FACE_ROWS = 160
 SX, SY, SZ, CY = 16, 4, 8, 8
 PLANE, ZLINE = 32, 16
 LOCAL_GAIN = (3 / 2.125) ** 0.5
@@ -72,13 +76,18 @@
 
 
 def kernel(body, probe, dens, links, offb, selfb, owner, state_out, adjoint_out, coarse_out,
-           x_first, x_rest, faces_first, faces_rest, pick, table, v, su, sc, rp, hot, rr, mp, mps, mz, mzs,
-           hs, hr, ps, pr, zs, zr):
+           x_first, x_rest, faces_first, faces_rest, low_own, low_far, vg, pick, table, v, su, sc, rp, hot, rr, mp, mps, mz, mzs,
+           hs, hr, fs, fr, ps, pr, zs, zr):
     gx, gy, gz = lax.axis_index("gx"), lax.axis_index("gy"), lax.axis_index("gz")
     zh, yc = gx // CY, gx % CY
     me_p = yc * SY + gy
     me_z = zh * SZ + gz
-    far = jnp.logical_or(gx == CY - 1, gx == CY)
+    ghost = jnp.logical_or(gx == CY - 1, gx == CY)
+    behind = jnp.logical_or(gx == CY - 2, gx == CY + 1)
+    mirror = (gx == CY).astype(jnp.int32)
+    across_peer = (2 * CY - 1 - gx, gy, gz)
+    behind_peer = (jnp.where(gx == CY + 1, CY - 1, CY), gy, gz)
+    greeter = (jnp.where(gx == CY, CY - 2, CY + 1), gy, gz)
 
     def plane_peer(i):
         p = (me_p + 1 + i) % PLANE
@@ -100,60 +109,136 @@
 
     lax.fori_loop(0, ZLINE - 1, greet_line, 0)
 
-    @pl.when(far)
-    def _():
-        pl.semaphore_signal(
-            barrier, inc=1, device_id=(2 * CY - 1 - gx, gy, gz), device_id_type=MESH
-        )
+    @pl.when(ghost)
+    def _():
+        for peer in (across_peer, greeter):
+            pl.semaphore_signal(barrier, inc=1, device_id=peer, device_id_type=MESH)
+
+    @pl.when(behind)
+    def _():
+        pl.semaphore_signal(barrier, inc=1, device_id=behind_peer, device_id_type=MESH)
 
     lax.fori_loop(0, PLANE - 1, greet_plane, 0)
 
     sends = (
-        (gx < SX - 1, (gx + 1, gy, gz)),
-        (gx > 0, (gx - 1, gy, gz)),
+        ((gx < SX - 1) & (gx != CY - 1), (gx + 1, gy, gz)),
+        ((gx > 0) & (gx != CY), (gx - 1, gy, gz)),
         (gy < SY - 1, (gx, gy + 1, gz)),
         (gy > 0, (gx, gy - 1, gz)),
         (gz < SZ - 1, (gx, gy, gz + 1)),
         (gz > 0, (gx, gy, gz - 1)),
     )
-    lands = ((LOWX, 32), (UPX, 32), (LOWY, 16), (UPY, 16), (LOWZ, 16), (UPZ, 16))
-    comes = tuple(sends[d ^ 1][0] for d in range(6))
-
-    def halo(k, d):
-        at, size = lands[d]
+    comes = (
+        (gx > 0) & (gx != CY),
+        (gx < SX - 1) & (gx != CY - 1),
+        gy > 0,
+        gy < SY - 1,
+        gz > 0,
+        gz < SZ - 1,
+    )
+    lands = (LOWX, jnp.where(gx == CY + 1, LOWX, UPX), LOWY, UPY, LOWZ, UPZ)
+    deep_rows = {0: (48, 32), 1: (32, 16), 2: (32, 16), 3: (16, 16)}
+
+    def rows_of(k, d, deep):
+        return deep_rows[k][(d - 2) // 2] if deep else 16
+
+    def halo(k, d, deep=False):
         x, faces = (x_first, faces_first) if k == 0 else (x_rest.at[k - 1], faces_rest.at[k - 1])
         if d < 2:
-            src = x.at[pl.ds(32 - 32 * d, 32)]
+            at = jnp.where(gx == CY, 0, LAYER) if d == 0 else 0
+            src = x.at[pl.ds(pl.multiple_of(at, LAYER), LAYER)]
+            dst = x.at[pl.ds(pl.multiple_of(lands[d], LAYER), LAYER)]
         else:
-            src = faces.at[pl.ds(16 * (d - 2), 16)]
+            size = rows_of(k, d, deep)
+            src = faces.at[pl.ds(FACES[d - 2], size)]
+            dst = x.at[pl.ds(lands[d], size)]
         return pltpu.make_async_remote_copy(
             src_ref=src,
-            dst_ref=x.at[pl.ds(at, size)],
+            dst_ref=dst,
             send_sem=hs.at[k, d],
             recv_sem=hr.at[k, d],
             device_id=sends[d][1],
             device_id_type=MESH,
         )
 
-    def start_halos(k):
-        for d in range(6):
-            @pl.when(sends[d][0])
-            def _():
-                halo(k, d).start()
-
-    def wait_halos(k):
-        for d in range(6):
-            @pl.when(comes[d])
-            def _():
-                halo(k, d).wait_recv()
-
-    for d in range(6):
-        at, size = lands[d]
-
-        @pl.when(jnp.logical_not(comes[d]))
+    def for_halos(k, ways, conditions, act):
+        for d in ways:
+            if d < 2:
+                @pl.when(conditions[d])
+                def _():
+                    act(halo(k, d))
+            else:
+                @pl.when(conditions[d] & ghost)
+                def _():
+                    act(halo(k, d, True))
+
+                @pl.when(conditions[d] & jnp.logical_not(ghost))
+                def _():
+                    act(halo(k, d, False))
+
+    def start_halos(k, ways=range(6)):
+        for_halos(k, ways, [c for c, _ in sends], lambda copy: copy.start())
+
+    def wait_halos(k, ways=range(6)):
+        for_halos(k, ways, comes, lambda copy: copy.wait_recv())
+
+    def far_copy(m):
+        first = jnp.where(gx == CY + 1, 0, LAYER)
+        src, dst, at, to = (
+            (x_first, x_first, LAYER, UPX),
+            (x_first, x_first, 0, UPX + LAYER),
+            (low_own, low_far, LAYER, 0),
+            (low_own, low_far, 0, LAYER),
+            (x_first, x_first, first, UPX + 2 * LAYER),
+            (x_first, x_first, LAYER - first, UPX + 3 * LAYER),
+            (low_own, low_far, first, 2 * LAYER),
+        )[m]
+        return pltpu.make_async_remote_copy(
+            src_ref=src.at[pl.ds(pl.multiple_of(at, LAYER), LAYER)],
+            dst_ref=dst.at[pl.ds(to, LAYER)],
+            send_sem=fs.at[m],
+            recv_sem=fr.at[m],
+            device_id=across_peer if m < 4 else behind_peer,
+            device_id_type=MESH,
+        )
+
+    def clear(at, size, first=True):
+        if first:
+            x_first[pl.ds(at, size), :] = jnp.zeros((size, 2 * LANES), BF16)
+        x_rest[:, pl.ds(at, size), :] = jnp.zeros((ITERS - 1, size, 4 * LANES), BF16)
+
+    clear(UPX + LAYER, 3 * LAYER, False)
+
+    @pl.when(jnp.logical_not(ghost))
+    def _():
+        x_first[pl.ds(UPX + LAYER, 3 * LAYER), :] = jnp.zeros((3 * LAYER, 2 * LANES), BF16)
+        low_far[...] = jnp.zeros(low_far.shape, BF16)
+        for at, size in ((LOWY, 48), (UPY, 48), (LOWZ, 32), (UPZ, 32)):
+            clear(at + 16, size - 16)
+
+    @pl.when(ghost)
+    def _():
+        for k in range(1, ITERS):
+            for d in range(2, 6):
+                size, full = deep_rows[k][(d - 2) // 2], deep_rows[0][(d - 2) // 2]
+                if size < full:
+                    x_rest[k - 1, pl.ds(lands[d] + size, full - size), :] = jnp.zeros(
+                        (full - size, 4 * LANES), BF16
+                    )
+
+    for absent, at, size in (
+        (gx == 0, LOWX, LAYER),
+        (gx == SX - 1, UPX, LAYER),
+        (gy == 0, LOWY, 48),
+        (gy == SY - 1, UPY, 48),
+        (gz == 0, LOWZ, 32),
+        (gz == SZ - 1, UPZ, 32),
+    ):
+        @pl.when(absent)
         def _():
-            x_first[pl.ds(at, size), :] = jnp.zeros((size, 2 * LANES), BF16)
-            x_rest[:, pl.ds(at, size), :] = jnp.zeros((ITERS - 1, size, 4 * LANES), BF16)
+            clear(at, size)
+
+    own = (mirror, 1 - mirror)
 
     eye8 = iota((8, 8), 0) == iota((8, 8), 1)
 
@@ -161,7 +246,7 @@
         return jnp.concatenate(
             [
                 jnp.sum(
-                    jnp.where(eye8, jnp.broadcast_to(row_of(a, b).astype(F32), (8, 8)), 0.0),
+                    jnp.where(eye8, jnp.broadcast_to(row_of(own[a], b).astype(F32), (8, 8)), 0.0),
                     axis=1,
                     keepdims=True,
                 )
@@ -175,112 +260,140 @@
     density = column(lambda a, b: dens[a, b : b + 1, :])
     owners = column(lambda a, b: owner[a, b : b + 1, :])
 
-    scale = density * jnp.sqrt(density)
     eye = iota((DOF, DOF), 0) == iota((DOF, DOF), 1)
     eye_low = jnp.where(eye, 1.0, 0.0).astype(BF16)
-    pivots = jnp.zeros((G, DOF), F32)
+    diagonals = []
     table[...] = jnp.zeros(table.shape, BF16)
     for t in range(4):
         block = selfb[t]
-        diagonal = jnp.sum(jnp.where(eye, block.astype(F32), 0.0), axis=0, keepdims=True)
-        pivots = jnp.where(kinds[6] == float(t), diagonal, pivots)
+        diagonals.append(
+            jnp.sum(jnp.where(eye, block.astype(F32), 0.0), axis=0, keepdims=True)
+        )
         upper = lax.dot_general(eye_low, offb[t], NT_DIMS, preferred_element_type=F32)
         table[pl.ds(t * LANES, DOF), pl.ds(0, DOF)] = upper.astype(BF16)
         table[pl.ds((4 + t) * LANES, DOF), pl.ds(0, DOF)] = offb[t]
         table[pl.ds((8 + t) * LANES, DOF), pl.ds(0, DOF)] = block
-    rp[...] = jnp.ones((G, LANES), F32)
-    rp[:, pl.ds(0, DOF)] = 1.0 / pivots
-    sc[...] = jnp.broadcast_to(scale, (G, LANES))
-    su[...] = rp[...] * sc[...]
+
+    def prepare(at, size, kinds, density):
+        scale = density * jnp.sqrt(density)
+        pivots = jnp.ones((size, DOF), F32)
+        for t in range(4):
+            pivots = jnp.where(kinds[6] == float(t), diagonals[t], pivots)
+        rows = pl.ds(at, size)
+        rp[rows, :] = jnp.ones((size, LANES), F32)
+        rp[rows, pl.ds(0, DOF)] = 1.0 / pivots
+        sc[rows, :] = jnp.broadcast_to(scale, (size, LANES))
+        su[rows, :] = rp[rows, :] * sc[rows, :]
+        g = iota((size, 1), 0) + at
+        gl, gyy, gzz = g // LAYER, g // NZ % NY, g % NZ
+        on = g + LAYER
+        back = jnp.where(gl == 0, LOWX + g, g - LAYER)
+        sources = (
+            jnp.where(mirror == 1, back, on),
+            jnp.where(gyy < NY - 1, g + 8, UPY + gl * 8 + gzz),
+            jnp.where(gzz < NZ - 1, g + 1, UPZ + gl * 4 + gyy),
+            jnp.where(mirror == 1, on, back),
+            jnp.where(gyy > 0, g - 8, LOWY + gl * 8 + gzz),
+            jnp.where(gzz > 0, g - 1, LOWZ + gl * 4 + gyy),
+        )
+        across = iota((size, ROWS), 1).astype(F32)
+        sources = [a.astype(F32) for a in sources]
+        for side in range(2):
+            for t in range(4):
+                chosen = jnp.zeros((size, ROWS), F32)
+                for k in range(3 * side, 3 * side + 3):
+                    code = jnp.where(kinds[k] == float(t), sources[k], -1.0)
+                    chosen = jnp.where(across == code, 1.0, chosen)
+                pick[pl.ds((4 * side + t) * ALL + at, size), :] = chosen.astype(BF16)
+        for t in range(4):
+            code = jnp.where(kinds[6] == float(t), g.astype(F32), -1.0)
+            pick[pl.ds((8 + t) * ALL + at, size), :] = jnp.where(across == code, 1.0, 0.0).astype(
+                BF16
+            )
+
+    prepare(0, G, kinds, density)
 
     v[0] = jnp.zeros((2 * G, LANES), F32)
-    v[0, pl.ds(0, G), pl.ds(0, DOF)] = body[...].reshape(G, DOF)
-    v[0, pl.ds(G, G), pl.ds(0, DOF)] = probe[...].reshape(G, DOF)
-
-    g = iota((G, 1), 0)
-    gl, gyy, gzz = g // 32, g // 8 % 4, g % 8
-    sources = (
-        jnp.where(gl == 0, g + 32, UPX + g - 32),
-        jnp.where(gyy < NY - 1, g + 8, UPY + gl * 8 + gzz),
-        jnp.where(gzz < NZ - 1, g + 1, UPZ + gl * 4 + gyy),
-        jnp.where(gl == 0, LOWX + g, g - 32),
-        jnp.where(gyy > 0, g - 8, LOWY + gl * 8 + gzz),
-        jnp.where(gzz > 0, g - 1, LOWZ + gl * 4 + gyy),
+    for a in range(NX):
+        for f, load in enumerate((body, probe)):
+            v[0, pl.ds(f * G + a * LAYER, LAYER), pl.ds(0, DOF)] = load[own[a]].reshape(LAYER, DOF)
+
+    r = iota((FACE_ROWS, 1), 0)
+    along_y, along_z = r % 48, r % 32
+    face_y = along_y // 8 * LAYER + along_y % 8
+    face_z = along_z // 4 * LAYER + along_z % 4 * 8
+    face = jnp.where(
+        r < 48, face_y + 24, jnp.where(r < 96, face_y, jnp.where(r < 128, face_z + 7, face_z))
     )
-    across = iota((G, ROWS), 1).astype(F32)
-    sources = [s.astype(F32) for s in sources]
-    for side in range(2):
-        for t in range(4):
-            chosen = jnp.zeros((G, ROWS), F32)
-            for k in range(3 * side, 3 * side + 3):
-                code = jnp.where(kinds[k] == float(t), sources[k], -1.0)
-                chosen = jnp.where(across == code, 1.0, chosen)
-            pick[pl.ds((4 * side + t) * G, G), :] = chosen.astype(BF16)
-    for t in range(4):
-        code = jnp.where(kinds[6] == float(t), g.astype(F32), -1.0)
-        pick[pl.ds((8 + t) * G, G), :] = jnp.where(across == code, 1.0, 0.0).astype(BF16)
-
-    r = iota((G, 1), 0)
-    r16 = r % 16
-    face_y = r16 // 8 * 32 + r16 % 8
-    face_z = jnp.where(r16 < 8, r16 // 4 * 32 + r16 % 4 * 8, -64)
-    face = jnp.where(
-        r < 16, face_y + 24, jnp.where(r < 32, face_y, jnp.where(r < 48, face_z + 7, face_z))
-    )
-    outer = jnp.where(iota((G, G), 1) == face, 1.0, 0.0).astype(BF16)
+    outer = jnp.where(iota((FACE_ROWS, ALL), 1) == face, 1.0, 0.0).astype(BF16)
 
     def both(a):
         return jnp.concatenate([a, a], axis=0)
 
-    def scaled(field, parts):
-        u = field * both(su[...])
+    def scaled(field, factor, parts):
+        size = factor.shape[0]
+        u = field * both(factor)
         high = u.astype(BF16)
-        out = [high[:G], high[G:]]
+        out = [high[:size], high[size:]]
         if parts == 2:
             low = (u - high.astype(F32)).astype(BF16)
-            out += [low[:G], low[G:]]
+            out += [low[:size], low[size:]]
         return jnp.concatenate(out, axis=1)
 
-    def wide(a, count):
+    def wide(a, size, count):
         return [
             jnp.concatenate(
-                [a[t * G : (t + 1) * G, f * LANES : (f + 1) * LANES] for t in range(count)],
+                [a[t * size : (t + 1) * size, f * LANES : (f + 1) * LANES] for t in range(count)],
                 axis=1,
             )
             for f in range(a.shape[1] // LANES)
         ]
 
-    def fold(a):
-        return a[: 2 * G] + a[2 * G :] if a.shape[0] == 4 * G else a
-
-    def image(sent, width, gain):
-        z = jnp.dot(pick[:, pl.ds(0, width)], sent, preferred_element_type=F32)
-        off, own = z[: 8 * G], z[8 * G :].astype(BF16)
+    def image(sent, size, width, gain):
+        def fold(a):
+            return a[: 2 * size] + a[2 * size :] if a.shape[0] == 4 * size else a
+
+        chosen = jnp.concatenate(
+            [pick[pl.ds(t * ALL, size), pl.ds(0, width)] for t in range(12)], axis=0
+        )
+        z = jnp.dot(chosen, sent, preferred_element_type=F32)
+        off, direct = z[: 8 * size], z[8 * size :].astype(BF16)
         if off.shape[1] == 4 * LANES:
             off = off[:, : 2 * LANES] + off[:, 2 * LANES :]
         high = off.astype(BF16)
         low = (off - high.astype(F32)).astype(BF16)
-        left = jnp.concatenate(wide(high, 8) + wide(low, 8), axis=0)
+        left = jnp.concatenate(wide(high, size, 8) + wide(low, size, 8), axis=0)
         a = jnp.dot(left, table[pl.ds(0, 8 * LANES)], preferred_element_type=F32)
         b = jnp.dot(
-            jnp.concatenate(wide(own, 4), axis=0),
+            jnp.concatenate(wide(direct, size, 4), axis=0),
             table[pl.ds(8 * LANES, 4 * LANES)],
             preferred_element_type=F32,
         )
         a = fold(a)
         if gain != 1.0:
             a = a * gain
-        return (a + fold(b)) * both(sc[...])
-
-    def ship(k, field):
-        sent = scaled(field, 1 if k == 0 else 2)
-        outside = jnp.dot(outer, sent, preferred_element_type=F32).astype(BF16)
-        if k == 0:
-            x_first[pl.ds(0, G), :] = sent
-            faces_first[...] = outside
-        else:
-            x_rest[k - 1, pl.ds(0, G), :] = sent
-            faces_rest[k - 1] = outside
+        return (a + fold(b)) * both(sc[pl.ds(0, size), :])
+
+    def faces_of(sent):
+        return jnp.dot(
+            outer[:, : sent.shape[0]], sent, preferred_element_type=F32
+        ).astype(BF16)
+
+    def ship(k):
+        more = (ITERS - k) * LAYER
+        sent = scaled(v[k], su[pl.ds(0, G), :], 2)
+        x_rest[k - 1, pl.ds(0, G), :] = sent
+        beyond = scaled(
+            jnp.concatenate([vg[f, pl.ds(0, more), :] for f in range(2)], axis=0),
+            su[pl.ds(G, more), :],
+            2,
+        )
+
+        @pl.when(ghost)
+        def _():
+            x_rest[k - 1, pl.ds(UPX, more), :] = beyond
+
+        faces_rest[k - 1] = faces_of(jnp.concatenate([sent, beyond], axis=0))
 
     def gram(fields, i, j):
         product = fields[i] * fields[j]
@@ -324,11 +437,29 @@
     rr[...] = jnp.zeros(rr.shape, F32)
     mp[...] = jnp.zeros(mp.shape, F32)
     mz[...] = jnp.zeros(mz.shape, F32)
-    ship(0, v[0])
+    sent = scaled(v[0], su[pl.ds(0, G), :], 2)
+    low_own[...] = sent[:, 2 * LANES :]
+
+    def split3(a):
+        first = a.astype(BF16).astype(F32)
+        second = (a - first).astype(BF16).astype(F32)
+        return [first, second, a - first - second]
+
+    lane = iota((G, LANES), 1)
+    notes = sent[:, :LANES].astype(F32)
+    for i, col in enumerate(kinds + split3(density)):
+        notes = jnp.where(lane == DOF + i, col, notes)
+    sent = jnp.concatenate([notes.astype(BF16), sent[:, LANES : 2 * LANES]], axis=1)
+    x_first[pl.ds(0, G), :] = sent
+
+    @pl.when(jnp.logical_not(ghost))
+    def _():
+        faces_first[...] = faces_of(sent)
+
 
     inner = [v[0]]
     for _ in range(ITERS - 1):
-        inner.append(image(scaled(inner[-1], 1), G, LOCAL_GAIN))
+        inner.append(image(scaled(inner[-1], su[pl.ds(0, G), :], 1), G, G, LOCAL_GAIN))
     for i in range(ITERS):
         for j in range(i, ITERS):
             gram(inner, i, j)
@@ -345,8 +476,28 @@
     mp[0, 2:3, :] = as_row(owners)
     mp[0, 3:4, :] = as_row(density)
 
-    pl.semaphore_wait(barrier, PLANE - 1 + ZLINE - 1 + far.astype(jnp.int32))
-    start_halos(0)
+    extra = 2 * ghost.astype(jnp.int32) + behind.astype(jnp.int32)
+    pl.semaphore_wait(barrier, PLANE - 1 + ZLINE - 1 + extra)
+
+    @pl.when(ghost)
+    def _():
+        for m in range(4):
+            far_copy(m).start()
+
+    @pl.when(behind)
+    def _():
+        for m in range(4, 7):
+            far_copy(m).start()
+
+    start_halos(0, (0, 1))
+
+    @pl.when(jnp.logical_not(ghost))
+    def _():
+        for d in range(2, 6):
+            @pl.when(sends[d][0])
+            def _():
+                halo(0, d).start()
+
     start_plane(0)
     wait_all(mps.at[0], pr.at[0])
     mz[0] = mp[0] + total(mps[0, i] for i in range(PLANE - 1))
@@ -378,11 +529,40 @@
 
     mz[1, 2:3, :] = by_block(0, 3)
 
+    wait_halos(0, (0, 1))
+
+    @pl.when(ghost)
+    def _():
+        for m in (0, 1, 4, 5):
+            far_copy(m).wait_recv()
+        faces_first[...] = faces_of(x_first[pl.ds(0, ALL), :])
+        for d in range(2, 6):
+            @pl.when(sends[d][0])
+            def _():
+                halo(0, d, True).start()
+
+    notes = x_first[pl.ds(UPX, DEEP * LAYER), pl.ds(128, 128)].astype(F32)
+    notes = [notes[:, DOF - 128 + i : DOF - 127 + i] for i in range(10)]
+    prepare(G, DEEP * LAYER, notes[:7], notes[7] + notes[8] + notes[9])
+
     guess = None
     for k in range(ITERS):
-        wait_halos(k)
-        moved = image(x_first[...] if k == 0 else x_rest[k - 1], ROWS, 1.0)
+        wait_halos(k, range(2, 6) if k == 0 else range(6))
+        size = ALL - k * LAYER
+        moved = image(x_first[...] if k == 0 else x_rest[k - 1], size, ROWS, 1.0)
+        ours = jnp.concatenate([moved[:G], moved[size : size + G]], axis=0)
         if k == 0:
+            @pl.when(ghost)
+            def _():
+                for m in (2, 3, 6):
+                    far_copy(m).wait_recv()
+
+            beyond = su[pl.ds(G, DEEP * LAYER), :]
+            beyond = jnp.where(beyond > 0.0, 1.0 / beyond, 0.0)
+            for f in range(2):
+                lanes = pl.ds(f * LANES, LANES)
+                whole = x_first[pl.ds(UPX, DEEP * LAYER), lanes].astype(F32)
+                vg[f] = (whole + low_far[:, lanes].astype(F32)) * beyond
             wait_all(mzs.at[0], zr.at[0])
             row = mz[0, 0:2, :] + total(mzs[0, i, 0:2, :] for i in range(ZLINE - 1))
             guess, _, _ = sweeps(
@@ -393,11 +573,17 @@
             step = jnp.concatenate(
                 [jnp.broadcast_to(guess[k][f : f + 1], (G, 1)) for f in range(2)], axis=0
             )
-            v[k + 1] = v[k] - step * moved
-            ship(k + 1, v[k + 1])
+            v[k + 1] = v[k] - step * ours
+            for f in range(2):
+                more = size - G
+                vg[f, pl.ds(0, more), :] = (
+                    vg[f, pl.ds(0, more), :]
+                    - guess[k][f : f + 1] * moved[f * size + G : (f + 1) * size]
+                )
+            ship(k + 1)
             start_halos(k + 1)
         else:
-            v[k + 1] = moved
+            v[k + 1] = ours
         for i in range(k + 2):
             gram(v, i, k + 1)
         if k == 0:
@@ -434,9 +620,10 @@
             c[f : f + 1, :] * v[i, pl.ds(f * G, G), :] for i, c in coefficients.items()
         )
 
-    solved = [combine(answer, f) * rp[...] for f in range(2)]
-    state_out[...] = solved[0][:, :DOF].reshape(state_out.shape)
-    adjoint_out[...] = solved[1][:, :DOF].reshape(adjoint_out.shape)
+    solved = [combine(answer, f) * rp[pl.ds(0, G), :] for f in range(2)]
+    for a in range(NX):
+        for f, out in enumerate((state_out, adjoint_out)):
+            out[own[a]] = solved[f][a * LAYER : (a + 1) * LAYER, :DOF].reshape(NY, NZ, DOF)
     applied = {i: (1.0 - c if i == 0 else -c) for i, c in left.items()}
     applied = [combine(applied, f) for f in range(2)]
     bracket = jnp.sum(solved[1] * applied[0] + solved[0] * applied[1], axis=1, keepdims=True)
@@ -454,10 +641,18 @@
     coarse_out[...] = jnp.sum(jnp.where(eye8, col, 0.0), axis=0, keepdims=True)
 
     for k in range(ITERS):
-        for d in range(6):
-            @pl.when(sends[d][0])
-            def _():
-                halo(k, d).wait_send()
+        for_halos(k, range(6), [c for c, _ in sends], lambda copy: copy.wait_send())
+
+    @pl.when(ghost)
+    def _():
+        for m in range(4):
+            far_copy(m).wait_send()
+
+    @pl.when(behind)
+    def _():
+        for m in range(4, 7):
+            far_copy(m).wait_send()
+
     for e in range(3):
         wait_all(mps.at[e], ps.at[e])
         wait_all(mzs.at[e], zs.at[e])
@@ -477,14 +672,17 @@
         scratch_shapes=[
             pltpu.VMEM((ROWS, 2 * LANES), BF16),
             pltpu.VMEM((ITERS - 1, ROWS, 4 * LANES), BF16),
+            pltpu.VMEM((FACE_ROWS, 2 * LANES), BF16),
+            pltpu.VMEM((ITERS - 1, FACE_ROWS, 4 * LANES), BF16),
             pltpu.VMEM((G, 2 * LANES), BF16),
-            pltpu.VMEM((ITERS - 1, G, 4 * LANES), BF16),
-            pltpu.VMEM((12 * G, ROWS), BF16),
+            pltpu.VMEM((DEEP * LAYER, 2 * LANES), BF16),
+            pltpu.VMEM((2, DEEP * LAYER, LANES), F32),
+            pltpu.VMEM((12 * ALL, ROWS), BF16),
             pltpu.VMEM((12 * LANES, LANES), BF16),
             pltpu.VMEM((ITERS + 1, 2 * G, LANES), F32),
-            pltpu.VMEM((G, LANES), F32),
-            pltpu.VMEM((G, LANES), F32),
-            pltpu.VMEM((G, LANES), F32),
+            pltpu.VMEM((ALL, LANES), F32),
+            pltpu.VMEM((ALL, LANES), F32),
+            pltpu.VMEM((ALL, LANES), F32),
             pltpu.VMEM((128, PLANE * G), BF16),
             pltpu.VMEM((32, 128), F32),
             pltpu.VMEM((3, 4, 128), F32),
@@ -493,6 +691,8 @@
             pltpu.VMEM((3, ZLINE - 1, 4, 128), F32),
             pltpu.SemaphoreType.DMA((ITERS, 6)),
             pltpu.SemaphoreType.DMA((ITERS, 6)),
+            pltpu.SemaphoreType.DMA((7,)),
+            pltpu.SemaphoreType.DMA((7,)),
             pltpu.SemaphoreType.DMA((3,)),
             pltpu.SemaphoreType.DMA((3,)),
             pltpu.SemaphoreType.DMA((3,)),

time: 91 us -> 91.6 us (level)
  no operation moved by 1% of the time
where the time goes in v2:
time: 91.6 us; the launch traced here: 91.4 us
  Pallas kernels  88.1 us (96%)
  local copies, waits for them, and re-layouts  2.65 us (3%)
    pallas_call x1, Pallas kernels, local(): pl.pallas_call(kernel, out_shape=(jax.ShapeDtypeStruct(body_load.shape, F...  88.1 us
    unnamed x7, local copies, waits for them, and re-layouts  2.65 us

profile of v2, /device:TPU:1, one launch (start us, length us, event | category | flops | bytes accessed | tf_op | source)
XLA Modules:
  0.0 91.4 jit_solution(7146505960268857892)
XLA Ops:
  0.6 88.1 %sweeps.1 = (f32[2,4,8,192]{3,2,1,0:T(8,128)}, f32[2,4,8,192]{3,2,1,0:T(8,128)}, f32[1,8]{1,0:T(1,128)}) custom-call(f32[2,4,8,192]{3,2,1,0:T(8,128)} %body.1, f32[2,4,8,192]{3,2,1,0:T(8,128)} %probe.1, f32[2,4,8]{2,1,0:T(4,128)} %dens.1, s32[2,7,4,8]{3,2,1,0:T(4,128)} %bitcast.2, bf16[4,192,192]{2,1,0:T(8,128)(2,1)} %offb.1, bf16[4,192,192]{2,1,0:T(8,128)(2,1)} %selfb.1, ...), custom_call_target="tpu_custom_call" | custom-call | tf_op jit(solution)/shard_map/sweeps/pallas_call | solution.py:663
  88.7 0.0 copy-start
  88.7 1.5 %copy.13 = f32[2,4,8,192]{3,2,1,0:T(8,128)} copy(f32[2,4,8,192]{3,2,1,0:T(8,128)} %get-tuple-element.12) | data formatting | bytes 98304
  90.2 0.0 copy-done
  90.2 0.0 copy-start.1
  90.3 0.6 copy.14
  90.9 0.0 copy-done.1
  90.9 0.5 copy.15
Async XLA Ops:
  88.7 1.5 %copy-start = (f32[2,4,8,192]{3,2,1,0:T(8,128)S(1)}, f32[2,4,8,192]{3,2,1,0:T(8,128)}, u32[]{:S(2)}) copy-start(f32[2,4,8,192]{3,2,1,0:T(8,128)} %get-tuple-element.13) | copy-start | bytes 147460
  90.2 0.6 copy-start.1

commit v3 on v2

--- a/solution.py
+++ b/solution.py
@@ -19,6 +19,7 @@
 UPX, LOWX, LOWY, UPY, LOWZ, UPZ, ROWS = 64, 192, 224, 272, 320, 352, 384
 FACES = (0, 48, 96, 128)
 FACE_ROWS = 160
+OUT, SOURCES = 96, 256
 SX, SY, SZ, CY = 16, 4, 8, 8
 PLANE, ZLINE = 32, 16
 LOCAL_GAIN = (3 / 2.125) ** 0.5
@@ -76,7 +77,7 @@
 
 
 def kernel(body, probe, dens, links, offb, selfb, owner, state_out, adjoint_out, coarse_out,
-           x_first, x_rest, faces_first, faces_rest, low_own, low_far, vg, pick, table, v, su, sc, rp, hot, rr, mp, mps, mz, mzs,
+           x_one, x_two, faces_one, faces_two, vg, pick, table, v, su, sc, rp, hot, rr, mp, mps, mz, mzs,
            hs, hr, fs, fr, ps, pr, zs, zr):
     gx, gy, gz = lax.axis_index("gx"), lax.axis_index("gy"), lax.axis_index("gz")
     zh, yc = gx // CY, gx % CY
@@ -143,7 +144,8 @@
         return deep_rows[k][(d - 2) // 2] if deep else 16
 
     def halo(k, d, deep=False):
-        x, faces = (x_first, faces_first) if k == 0 else (x_rest.at[k - 1], faces_rest.at[k - 1])
+        x = x_one.at[k] if k < 2 else x_two.at[k - 2]
+        faces = faces_one.at[k] if k < 2 else faces_two.at[k - 2]
         if d < 2:
             at = jnp.where(gx == CY, 0, LAYER) if d == 0 else 0
             src = x.at[pl.ds(pl.multiple_of(at, LAYER), LAYER)]
@@ -184,35 +186,26 @@
 
     def far_copy(m):
         first = jnp.where(gx == CY + 1, 0, LAYER)
-        src, dst, at, to = (
-            (x_first, x_first, LAYER, UPX),
-            (x_first, x_first, 0, UPX + LAYER),
-            (low_own, low_far, LAYER, 0),
-            (low_own, low_far, 0, LAYER),
-            (x_first, x_first, first, UPX + 2 * LAYER),
-            (x_first, x_first, LAYER - first, UPX + 3 * LAYER),
-            (low_own, low_far, first, 2 * LAYER),
-        )[m]
+        at = (LAYER, 0, first, LAYER - first)[m]
         return pltpu.make_async_remote_copy(
-            src_ref=src.at[pl.ds(pl.multiple_of(at, LAYER), LAYER)],
-            dst_ref=dst.at[pl.ds(to, LAYER)],
+            src_ref=x_one.at[0, pl.ds(pl.multiple_of(at, LAYER), LAYER)],
+            dst_ref=x_one.at[0, pl.ds(UPX + m * LAYER, LAYER)],
             send_sem=fs.at[m],
             recv_sem=fr.at[m],
-            device_id=across_peer if m < 4 else behind_peer,
+            device_id=across_peer if m < 2 else behind_peer,
             device_id_type=MESH,
         )
 
     def clear(at, size, first=True):
-        if first:
-            x_first[pl.ds(at, size), :] = jnp.zeros((size, 2 * LANES), BF16)
-        x_rest[:, pl.ds(at, size), :] = jnp.zeros((ITERS - 1, size, 4 * LANES), BF16)
+        for k in range(0 if first else 1, 2):
+            x_one[k, pl.ds(at, size), :] = jnp.zeros((size, 2 * LANES), BF16)
+        x_two[:, pl.ds(at, size), :] = jnp.zeros((2, size, 4 * LANES), BF16)
 
     clear(UPX + LAYER, 3 * LAYER, False)
 
     @pl.when(jnp.logical_not(ghost))
     def _():
-        x_first[pl.ds(UPX + LAYER, 3 * LAYER), :] = jnp.zeros((3 * LAYER, 2 * LANES), BF16)
-        low_far[...] = jnp.zeros(low_far.shape, BF16)
+        x_one[0, pl.ds(UPX + LAYER, 3 * LAYER), :] = jnp.zeros((3 * LAYER, 2 * LANES), BF16)
         for at, size in ((LOWY, 48), (UPY, 48), (LOWZ, 32), (UPZ, 32)):
             clear(at + 16, size - 16)
 
@@ -222,9 +215,11 @@
             for d in range(2, 6):
                 size, full = deep_rows[k][(d - 2) // 2], deep_rows[0][(d - 2) // 2]
                 if size < full:
-                    x_rest[k - 1, pl.ds(lands[d] + size, full - size), :] = jnp.zeros(
-                        (full - size, 4 * LANES), BF16
-                    )
+                    rest = pl.ds(lands[d] + size, full - size)
+                    if k < 2:
+                        x_one[k, rest, :] = jnp.zeros((full - size, 2 * LANES), BF16)
+                    else:
+                        x_two[k - 2, rest, :] = jnp.zeros((full - size, 4 * LANES), BF16)
 
     for absent, at, size in (
         (gx == 0, LOWX, LAYER),
@@ -285,31 +280,30 @@
         sc[rows, :] = jnp.broadcast_to(scale, (size, LANES))
         su[rows, :] = rp[rows, :] * sc[rows, :]
         g = iota((size, 1), 0) + at
-        gl, gyy, gzz = g // LAYER, g // NZ % NY, g % NZ
-        on = g + LAYER
-        back = jnp.where(gl == 0, LOWX + g, g - LAYER)
+        gl, here, gyy, gzz = g // LAYER, g % LAYER, g // NZ % NY, g % NZ
+        on, back = here + 2 * LAYER, here
+        y, z = OUT + gl * NZ + gzz, OUT + gl * NY + gyy
         sources = (
             jnp.where(mirror == 1, back, on),
-            jnp.where(gyy < NY - 1, g + 8, UPY + gl * 8 + gzz),
-            jnp.where(gzz < NZ - 1, g + 1, UPZ + gl * 4 + gyy),
+            jnp.where(gyy < NY - 1, here + LAYER + 8, y + FACES[1]),
+            jnp.where(gzz < NZ - 1, here + LAYER + 1, z + FACES[3]),
             jnp.where(mirror == 1, on, back),
-            jnp.where(gyy > 0, g - 8, LOWY + gl * 8 + gzz),
-            jnp.where(gzz > 0, g - 1, LOWZ + gl * 4 + gyy),
-        )
-        across = iota((size, ROWS), 1).astype(F32)
+            jnp.where(gyy > 0, here + LAYER - 8, y + FACES[0]),
+            jnp.where(gzz > 0, here + LAYER - 1, z + FACES[2]),
+        )
+        across = iota((size, SOURCES), 1).astype(F32)
         sources = [a.astype(F32) for a in sources]
         for side in range(2):
             for t in range(4):
-                chosen = jnp.zeros((size, ROWS), F32)
+                chosen = jnp.zeros((size, SOURCES), F32)
                 for k in range(3 * side, 3 * side + 3):
                     code = jnp.where(kinds[k] == float(t), sources[k], -1.0)
                     chosen = jnp.where(across == code, 1.0, chosen)
-                pick[pl.ds((4 * side + t) * ALL + at, size), :] = chosen.astype(BF16)
-        for t in range(4):
-            code = jnp.where(kinds[6] == float(t), g.astype(F32), -1.0)
-            pick[pl.ds((8 + t) * ALL + at, size), :] = jnp.where(across == code, 1.0, 0.0).astype(
-                BF16
-            )
+                chosen = chosen.astype(BF16)
+                for i in range(size // LAYER):
+                    pick[at // LAYER + i, pl.ds((4 * side + t) * LAYER, LAYER), :] = chosen[
+                        i * LAYER : (i + 1) * LAYER
+                    ]
 
     prepare(0, G, kinds, density)
 
@@ -338,41 +332,62 @@
         if parts == 2:
             low = (u - high.astype(F32)).astype(BF16)
             out += [low[:size], low[size:]]
-        return jnp.concatenate(out, axis=1)
-
-    def wide(a, size, count):
-        return [
-            jnp.concatenate(
-                [a[t * size : (t + 1) * size, f * LANES : (f + 1) * LANES] for t in range(count)],
-                axis=1,
+        return out
+
+    def fold(a, size):
+        return a[: 2 * size] + a[2 * size :] if a.shape[0] == 4 * size else a
+
+    def straight(parts, kind):
+        size = kind.shape[0]
+        masks = [jnp.broadcast_to(kind == float(t), (size, LANES)) for t in range(4)]
+        left = []
+        for part in parts:
+            part = part.astype(F32)
+            left.append(
+                jnp.concatenate([jnp.where(m, part, 0.0).astype(BF16) for m in masks], axis=1)
             )
-            for f in range(a.shape[1] // LANES)
-        ]
-
-    def image(sent, size, width, gain):
-        def fold(a):
-            return a[: 2 * size] + a[2 * size :] if a.shape[0] == 4 * size else a
-
-        chosen = jnp.concatenate(
-            [pick[pl.ds(t * ALL, size), pl.ds(0, width)] for t in range(12)], axis=0
-        )
-        z = jnp.dot(chosen, sent, preferred_element_type=F32)
-        off, direct = z[: 8 * size], z[8 * size :].astype(BF16)
-        if off.shape[1] == 4 * LANES:
-            off = off[:, : 2 * LANES] + off[:, 2 * LANES :]
-        high = off.astype(BF16)
-        low = (off - high.astype(F32)).astype(BF16)
-        left = jnp.concatenate(wide(high, size, 8) + wide(low, size, 8), axis=0)
-        a = jnp.dot(left, table[pl.ds(0, 8 * LANES)], preferred_element_type=F32)
-        b = jnp.dot(
-            jnp.concatenate(wide(direct, size, 4), axis=0),
-            table[pl.ds(8 * LANES, 4 * LANES)],
-            preferred_element_type=F32,
-        )
-        a = fold(a)
-        if gain != 1.0:
-            a = a * gain
-        return (a + fold(b)) * both(sc[pl.ds(0, size), :])
+        left = jnp.concatenate(left, axis=0)
+        return fold(
+            jnp.dot(left, table[pl.ds(8 * LANES, 4 * LANES)], preferred_element_type=F32), size
+        )
+
+    def coupled(sources):
+        size = len(sources) * LAYER
+        highs, lows = ([], []), ([], [])
+        for i, source in enumerate(sources):
+            z = jnp.dot(pick[i], source, preferred_element_type=F32)
+            if z.shape[1] == 4 * LANES:
+                z = z[:, : 2 * LANES] + z[:, 2 * LANES :]
+            high = z.astype(BF16)
+            low = (z - high.astype(F32)).astype(BF16)
+            for f in range(2):
+                for a, out in ((high, highs), (low, lows)):
+                    out[f].append(
+                        jnp.concatenate(
+                            [
+                                a[t * LAYER : (t + 1) * LAYER, f * LANES : (f + 1) * LANES]
+                                for t in range(8)
+                            ],
+                            axis=1,
+                        )
+                    )
+        left = jnp.concatenate(highs[0] + highs[1] + lows[0] + lows[1], axis=0)
+        return fold(jnp.dot(left, table[pl.ds(0, 8 * LANES)], preferred_element_type=F32), size)
+
+    def sources_of(k, layers):
+        def rows(at, size):
+            return x_one[k, pl.ds(at, size), :] if k < 2 else x_two[k - 2, pl.ds(at, size), :]
+
+        outside = rows(LOWY, FACE_ROWS)
+        out = []
+        for i in range(layers):
+            near = (
+                [rows(LOWX, LAYER), rows(0, 2 * LAYER)]
+                if i == 0
+                else [rows((i - 1) * LAYER, 3 * LAYER)]
+            )
+            out.append(jnp.concatenate(near + [outside], axis=0))
+        return out
 
     def faces_of(sent):
         return jnp.dot(
@@ -381,19 +396,29 @@
 
     def ship(k):
         more = (ITERS - k) * LAYER
-        sent = scaled(v[k], su[pl.ds(0, G), :], 2)
-        x_rest[k - 1, pl.ds(0, G), :] = sent
-        beyond = scaled(
+        own_parts = scaled(v[k], su[pl.ds(0, G), :], 1 if k < 2 else 2)
+        far_parts = scaled(
             jnp.concatenate([vg[f, pl.ds(0, more), :] for f in range(2)], axis=0),
             su[pl.ds(G, more), :],
-            2,
-        )
+            1 if k < 2 else 2,
+        )
+        sent = jnp.concatenate(own_parts, axis=1)
+        beyond = jnp.concatenate(far_parts, axis=1)
+        x, i = (x_one, k) if k < 2 else (x_two, k - 2)
+        x[i, pl.ds(0, G), :] = sent
 
         @pl.when(ghost)
         def _():
-            x_rest[k - 1, pl.ds(UPX, more), :] = beyond
-
-        faces_rest[k - 1] = faces_of(jnp.concatenate([sent, beyond], axis=0))
+            x[i, pl.ds(UPX, more), :] = beyond
+
+        (faces_one if k < 2 else faces_two)[i] = faces_of(
+            jnp.concatenate([sent, beyond], axis=0)
+        )
+        last = more - LAYER
+        return [
+            jnp.concatenate([a, b[:last]], axis=0) if last else a
+            for a, b in zip(own_parts, far_parts)
+        ]
 
     def gram(fields, i, j):
         product = fields[i] * fields[j]
@@ -437,8 +462,7 @@
     rr[...] = jnp.zeros(rr.shape, F32)
     mp[...] = jnp.zeros(mp.shape, F32)
     mz[...] = jnp.zeros(mz.shape, F32)
-    sent = scaled(v[0], su[pl.ds(0, G), :], 2)
-    low_own[...] = sent[:, 2 * LANES :]
+    sent = scaled(v[0], su[pl.ds(0, G), :], 1)
 
     def split3(a):
         first = a.astype(BF16).astype(F32)
@@ -446,20 +470,32 @@
         return [first, second, a - first - second]
 
     lane = iota((G, LANES), 1)
-    notes = sent[:, :LANES].astype(F32)
+    notes = sent[0].astype(F32)
     for i, col in enumerate(kinds + split3(density)):
         notes = jnp.where(lane == DOF + i, col, notes)
-    sent = jnp.concatenate([notes.astype(BF16), sent[:, LANES : 2 * LANES]], axis=1)
-    x_first[pl.ds(0, G), :] = sent
+    sent = jnp.concatenate([notes.astype(BF16), sent[1]], axis=1)
+    x_one[0, pl.ds(0, G), :] = sent
 
     @pl.when(jnp.logical_not(ghost))
     def _():
-        faces_first[...] = faces_of(sent)
+        faces_one[0] = faces_of(sent)
 
 
     inner = [v[0]]
     for _ in range(ITERS - 1):
-        inner.append(image(scaled(inner[-1], su[pl.ds(0, G), :], 1), G, G, LOCAL_GAIN))
+        parts = scaled(inner[-1], su[pl.ds(0, G), :], 1)
+        near = jnp.concatenate(parts, axis=1)
+
+        def empty(size):
+            return jnp.zeros((size, 2 * LANES), BF16)
+
+        moved = LOCAL_GAIN * coupled(
+            [
+                jnp.concatenate([empty(LAYER), near, empty(FACE_ROWS)], axis=0),
+                jnp.concatenate([near, empty(LAYER + FACE_ROWS)], axis=0),
+            ]
+        )
+        inner.append((moved + straight(parts, kinds[6])) * both(sc[pl.ds(0, G), :]))
     for i in range(ITERS):
         for j in range(i, ITERS):
             gram(inner, i, j)
@@ -481,12 +517,12 @@
 
     @pl.when(ghost)
     def _():
-        for m in range(4):
+        for m in range(2):
             far_copy(m).start()
 
     @pl.when(behind)
     def _():
-        for m in range(4, 7):
+        for m in range(2, 4):
             far_copy(m).start()
 
     start_halos(0, (0, 1))
@@ -533,36 +569,33 @@
 
     @pl.when(ghost)
     def _():
-        for m in (0, 1, 4, 5):
+        for m in range(4):
             far_copy(m).wait_recv()
-        faces_first[...] = faces_of(x_first[pl.ds(0, ALL), :])
+        faces_one[0] = faces_of(x_one[0, pl.ds(0, ALL), :])
         for d in range(2, 6):
             @pl.when(sends[d][0])
             def _():
                 halo(0, d, True).start()
 
-    notes = x_first[pl.ds(UPX, DEEP * LAYER), pl.ds(128, 128)].astype(F32)
+    notes = x_one[0, pl.ds(UPX, DEEP * LAYER), pl.ds(128, 128)].astype(F32)
     notes = [notes[:, DOF - 128 + i : DOF - 127 + i] for i in range(10)]
     prepare(G, DEEP * LAYER, notes[:7], notes[7] + notes[8] + notes[9])
+    kind = jnp.concatenate([kinds[6], notes[6]], axis=0)
+    beyond = su[pl.ds(G, DEEP * LAYER), :]
+    beyond = jnp.where(beyond > 0.0, 1.0 / beyond, 0.0)
+    parts = []
+    for f in range(2):
+        parts.append(x_one[0, pl.ds(0, ALL), pl.ds(f * LANES, LANES)])
+        vg[f] = parts[f][G:].astype(F32) * beyond
 
     guess = None
     for k in range(ITERS):
+        size = ALL - k * LAYER
+        alone = straight(parts, kind[:size])
         wait_halos(k, range(2, 6) if k == 0 else range(6))
-        size = ALL - k * LAYER
-        moved = image(x_first[...] if k == 0 else x_rest[k - 1], size, ROWS, 1.0)
+        moved = (coupled(sources_of(k, size // LAYER)) + alone) * both(sc[pl.ds(0, size), :])
         ours = jnp.concatenate([moved[:G], moved[size : size + G]], axis=0)
         if k == 0:
-            @pl.when(ghost)
-            def _():
-                for m in (2, 3, 6):
-                    far_copy(m).wait_recv()
-
-            beyond = su[pl.ds(G, DEEP * LAYER), :]
-            beyond = jnp.where(beyond > 0.0, 1.0 / beyond, 0.0)
-            for f in range(2):
-                lanes = pl.ds(f * LANES, LANES)
-                whole = x_first[pl.ds(UPX, DEEP * LAYER), lanes].astype(F32)
-                vg[f] = (whole + low_far[:, lanes].astype(F32)) * beyond
             wait_all(mzs.at[0], zr.at[0])
             row = mz[0, 0:2, :] + total(mzs[0, i, 0:2, :] for i in range(ZLINE - 1))
             guess, _, _ = sweeps(
@@ -580,7 +613,7 @@
                     vg[f, pl.ds(0, more), :]
                     - guess[k][f : f + 1] * moved[f * size + G : (f + 1) * size]
                 )
-            ship(k + 1)
+            parts = ship(k + 1)
             start_halos(k + 1)
         else:
             v[k + 1] = ours
@@ -645,12 +678,12 @@
 
     @pl.when(ghost)
     def _():
-        for m in range(4):
+        for m in range(2):
             far_copy(m).wait_send()
 
     @pl.when(behind)
     def _():
-        for m in range(4, 7):
+        for m in range(2, 4):
             far_copy(m).wait_send()
 
     for e in range(3):
@@ -670,14 +703,12 @@
         in_specs=[vmem] * 7,
         out_specs=(vmem,) * 3,
         scratch_shapes=[
-            pltpu.VMEM((ROWS, 2 * LANES), BF16),
-            pltpu.VMEM((ITERS - 1, ROWS, 4 * LANES), BF16),
-            pltpu.VMEM((FACE_ROWS, 2 * LANES), BF16),
-            pltpu.VMEM((ITERS - 1, FACE_ROWS, 4 * LANES), BF16),
-            pltpu.VMEM((G, 2 * LANES), BF16),
-            pltpu.VMEM((DEEP * LAYER, 2 * LANES), BF16),
+            pltpu.VMEM((2, ROWS, 2 * LANES), BF16),
+            pltpu.VMEM((2, ROWS, 4 * LANES), BF16),
+            pltpu.VMEM((2, FACE_ROWS, 2 * LANES), BF16),
+            pltpu.VMEM((2, FACE_ROWS, 4 * LANES), BF16),
             pltpu.VMEM((2, DEEP * LAYER, LANES), F32),
-            pltpu.VMEM((12 * ALL, ROWS), BF16),
+            pltpu.VMEM((5, 8 * LAYER, SOURCES), BF16),
             pltpu.VMEM((12 * LANES, LANES), BF16),
             pltpu.VMEM((ITERS + 1, 2 * G, LANES), F32),
             pltpu.VMEM((ALL, LANES), F32),
@@ -691,8 +722,8 @@
             pltpu.VMEM((3, ZLINE - 1, 4, 128), F32),
             pltpu.SemaphoreType.DMA((ITERS, 6)),
             pltpu.SemaphoreType.DMA((ITERS, 6)),
-            pltpu.SemaphoreType.DMA((7,)),
-            pltpu.SemaphoreType.DMA((7,)),
+            pltpu.SemaphoreType.DMA((4,)),
+            pltpu.SemaphoreType.DMA((4,)),
             pltpu.SemaphoreType.DMA((3,)),
             pltpu.SemaphoreType.DMA((3,)),
             pltpu.SemaphoreType.DMA((3,)),

time: 91.6 us -> 80.7 us (0.88)
  Pallas kernels: 88.1 us -> 77.2 us
    pallas_call x1, Pallas kernels: 88.1 us -> 77.2 us  [local(): pl.pallas_call(kernel, out_shape=(jax.ShapeDtypeStruct(body_load.shape, F...]
where the time goes in v3:
time: 80.7 us; the launch traced here: 80.5 us
  Pallas kernels  77.2 us (96%)
  local copies, waits for them, and re-layouts  2.65 us (3%)
    pallas_call x1, Pallas kernels, local(): pl.pallas_call(kernel, out_shape=(jax.ShapeDtypeStruct(body_load.shape, F...  77.2 us
    unnamed x7, local copies, waits for them, and re-layouts  2.65 us

profile of v3, /device:TPU:1, one launch (start us, length us, event | category | flops | bytes accessed | tf_op | source)
XLA Modules:
  0.0 80.5 jit_solution(12926909465135580449)
XLA Ops:
  0.6 77.2 %sweeps.1 = (f32[2,4,8,192]{3,2,1,0:T(8,128)}, f32[2,4,8,192]{3,2,1,0:T(8,128)}, f32[1,8]{1,0:T(1,128)}) custom-call(f32[2,4,8,192]{3,2,1,0:T(8,128)} %body.1, f32[2,4,8,192]{3,2,1,0:T(8,128)} %probe.1, f32[2,4,8]{2,1,0:T(4,128)} %dens.1, s32[2,7,4,8]{3,2,1,0:T(4,128)} %bitcast.2, bf16[4,192,192]{2,1,0:T(8,128)(2,1)} %offb.1, bf16[4,192,192]{2,1,0:T(8,128)(2,1)} %selfb.1, ...), custom_call_target="tpu_custom_call" | custom-call | tf_op jit(solution)/shard_map/sweeps/pallas_call | solution.py:696
  77.8 0.0 copy-start
  77.8 1.5 %copy.13 = f32[2,4,8,192]{3,2,1,0:T(8,128)} copy(f32[2,4,8,192]{3,2,1,0:T(8,128)} %get-tuple-element.12) | data formatting | bytes 98304
  79.4 0.0 copy-done
  79.4 0.0 copy-start.1
  79.4 0.6 copy.14
  80.0 0.0 copy-done.1
  80.0 0.5 copy.15
Async XLA Ops:
  77.8 1.5 %copy-start = (f32[2,4,8,192]{3,2,1,0:T(8,128)S(1)}, f32[2,4,8,192]{3,2,1,0:T(8,128)}, u32[]{:S(2)}) copy-start(f32[2,4,8,192]{3,2,1,0:T(8,128)} %get-tuple-element.13) | copy-start | bytes 147460
  79.4 0.6 copy-start.1

commit v4 on v3

--- a/solution.py
+++ b/solution.py
@@ -77,7 +77,7 @@
 
 
 def kernel(body, probe, dens, links, offb, selfb, owner, state_out, adjoint_out, coarse_out,
-           x_one, x_two, faces_one, faces_two, vg, pick, table, v, su, sc, rp, hot, rr, mp, mps, mz, mzs,
+           x_one, x_two, faces_one, faces_two, vg, pick, table, v, su, sc, rp, hot, rr, mp, mps, mz, mzs, mq, mqs, split, tile, tiles,
            hs, hr, fs, fr, ps, pr, zs, zr):
     gx, gy, gz = lax.axis_index("gx"), lax.axis_index("gy"), lax.axis_index("gz")
     zh, yc = gx // CY, gx % CY
@@ -436,9 +436,12 @@
 
     def start_plane(e):
         def one(i, _):
+            if e == 0:
+                src, dst = mp, mps.at[PLANE - 2 - i]
+            else:
+                src, dst = mq, mqs.at[PLANE - 2 - i]
             pltpu.make_async_remote_copy(
-                src_ref=mp.at[e], dst_ref=mps.at[e, PLANE - 2 - i],
-                send_sem=ps.at[e], recv_sem=pr.at[e],
+                src_ref=src, dst_ref=dst, send_sem=ps.at[e], recv_sem=pr.at[e],
                 device_id=plane_peer(i), device_id_type=MESH,
             ).start()
             return 0
@@ -446,22 +449,21 @@
         lax.fori_loop(0, PLANE - 1, one, 0)
 
     def start_line(e):
-        def one(i, _):
+        for o in sorted(range(1, ZLINE), key=lambda o: -min(o, ZLINE - o)):
+            i = o - 1
+            if e == 0:
+                src, dst = mz, mzs.at[ZLINE - 2 - i]
+            else:
+                src, dst = tile.at[(me_z + o) % ZLINE], tiles.at[ZLINE - 2 - i]
             pltpu.make_async_remote_copy(
-                src_ref=mz.at[e], dst_ref=mzs.at[e, ZLINE - 2 - i],
-                send_sem=zs.at[e], recv_sem=zr.at[e],
+                src_ref=src, dst_ref=dst, send_sem=zs.at[e], recv_sem=zr.at[e],
                 device_id=line_peer(i), device_id_type=MESH,
             ).start()
-            return 0
-
-        lax.fori_loop(0, ZLINE - 1, one, 0)
 
     def wait_all(buffer, sem):
         pltpu.make_async_copy(buffer, buffer, sem).wait()
 
     rr[...] = jnp.zeros(rr.shape, F32)
-    mp[...] = jnp.zeros(mp.shape, F32)
-    mz[...] = jnp.zeros(mz.shape, F32)
     sent = scaled(v[0], su[pl.ds(0, G), :], 1)
 
     def split3(a):
@@ -500,17 +502,16 @@
         for j in range(i, ITERS):
             gram(inner, i, j)
 
-    half = G * (me_p % 2)
-    spread = iota((G, 128), 1) == iota((G, 128), 0) + half
+    spread = iota((G, 128), 1) == iota((G, 128), 0)
 
     def as_row(col):
         return jnp.sum(jnp.where(spread, col, 0.0), axis=0, keepdims=True)
 
     rows = gram_rows()
-    mp[0, 0:1, :] = rows[0]
-    mp[0, 1:2, :] = rows[1]
-    mp[0, 2:3, :] = as_row(owners)
-    mp[0, 3:4, :] = as_row(density)
+    mp[0:1, :] = rows[0]
+    mp[1:2, :] = rows[1]
+    mp[2:3, :] = as_row(owners)
+    mp[3:4, :] = as_row(density)
 
     extra = 2 * ghost.astype(jnp.int32) + behind.astype(jnp.int32)
     pl.semaphore_wait(barrier, PLANE - 1 + ZLINE - 1 + extra)
@@ -535,35 +536,28 @@
                 halo(0, d).start()
 
     start_plane(0)
-    wait_all(mps.at[0], pr.at[0])
-    mz[0] = mp[0] + total(mps[0, i] for i in range(PLANE - 1))
+    wait_all(mps, pr.at[0])
+    mz[...] = mp[...] + total(mps[i] for i in range(PLANE - 1))
     start_line(0)
 
-    def gathered(e, row):
-        parts = [mps[e, i, row : row + 1, :] for i in range(PLANE - 1)]
-        parts.append(mp[e, row : row + 1, :])
-        return [parts[2 * m] + parts[2 * m + 1] for m in range(PLANE // 2)]
+    low_half = iota((1, 128), 1) < G
+
+    def joined(a, b):
+        return jnp.where(low_half, a, pltpu.roll(b, G, 1))
+
+    def gathered(row):
+        parts = [mps[i, row : row + 1, :] for i in range(PLANE - 1)]
+        parts.append(mp[row : row + 1, :])
+        return [joined(parts[2 * m], parts[2 * m + 1]) for m in range(PLANE // 2)]
 
     q = iota((128, 1), 0)
     bins = (((q // 64 * CY + yc) * SY + gy) * SZ + q // 8 % 8) * GPB + q % 8
     bins = bins.astype(F32)
-    for m, row in enumerate(gathered(0, 2)):
+    for m, row in enumerate(gathered(2)):
         hot[:, pl.ds(m * 128, 128)] = jnp.where(row == bins, 1.0, 0.0).astype(BF16)
 
-    def by_block(e, row):
-        flat = jnp.concatenate(gathered(e, row), axis=1)
-        first = flat.astype(BF16).astype(F32)
-        rest = flat - first
-        second = rest.astype(BF16).astype(F32)
-        third = rest - second
-        sub = iota((8, flat.shape[1]), 0)
-        split = jnp.where(
-            sub == 0, first, jnp.where(sub == 1, second, jnp.where(sub == 2, third, 0.0))
-        ).astype(BF16)
-        sums = lax.dot_general(split, hot[...], NT_DIMS, preferred_element_type=F32)
-        return jnp.sum(sums, axis=0, keepdims=True)
-
-    mz[1, 2:3, :] = by_block(0, 3)
+    masses = gathered(3)
+    split[pl.ds(96, 32), :] = jnp.zeros((32, PLANE * G), BF16)
 
     wait_halos(0, (0, 1))
 
@@ -588,6 +582,19 @@
         parts.append(x_one[0, pl.ds(0, ALL), pl.ds(f * LANES, LANES)])
         vg[f] = parts[f][G:].astype(F32) * beyond
 
+    spots = {}
+    for i in range(ITERS + 1):
+        for j in range(ITERS + 1):
+            if i + j < 2 * ITERS:
+                spots[i, j] = len(spots) % 12 + 16 * (len(spots) // 12)
+    lane = iota((G, 128), 1)
+    columns = [jnp.zeros((G, 128), F32)]
+
+    def products(i, j):
+        part = v[i, pl.ds(G, G), :] * rp[pl.ds(0, G), :] * v[j, pl.ds(0, G), :]
+        col = jnp.sum(part, axis=1, keepdims=True)
+        columns[0] = jnp.where(lane == spots[i, j], col, columns[0])
+
     guess = None
     for k in range(ITERS):
         size = ALL - k * LAYER
@@ -596,8 +603,8 @@
         moved = (coupled(sources_of(k, size // LAYER)) + alone) * both(sc[pl.ds(0, size), :])
         ours = jnp.concatenate([moved[:G], moved[size : size + G]], axis=0)
         if k == 0:
-            wait_all(mzs.at[0], zr.at[0])
-            row = mz[0, 0:2, :] + total(mzs[0, i, 0:2, :] for i in range(ZLINE - 1))
+            wait_all(mzs, zr.at[0])
+            row = mz[0:2, :] + total(mzs[i, 0:2, :] for i in range(ZLINE - 1))
             guess, _, _ = sweeps(
                 entries(row, ITERS), ITERS - 1, lambda c: {i + 1: e for i, e in c.items()}
             )
@@ -621,17 +628,48 @@
             gram(v, i, k + 1)
         if k == 0:
             gram(v, 0, 0)
+            products(0, 0)
+        for i in range(k + 1):
+            products(i, k + 1)
+            products(k + 1, i)
+        if 0 < k + 1 < ITERS:
+            products(k + 1, k + 1)
 
     rows = gram_rows()
-    mp[1, 0:1, :] = rows[0]
-    mp[1, 1:2, :] = rows[1]
+    turned = jnp.transpose(jnp.concatenate([columns[0], jnp.zeros((G, 128), F32)], axis=0))
+    mq[...] = jnp.where(low_half, turned[0:16], pltpu.roll(turned[16:32], G, 1))
+    mq[12:13, :] = rows[0]
+    mq[13:14, :] = rows[1]
     start_plane(1)
-    wait_all(mps.at[1], pr.at[1])
-    mz[1, 0:2, :] = mp[1, 0:2, :] + total(mps[1, i, 0:2, :] for i in range(PLANE - 1))
+    wait_all(mqs, pr.at[1])
+    sums = mq[12:14, :] + total(mqs[i, 12:14, :] for i in range(PLANE - 1))
+    sub = iota((16, 128), 0)
+    for m in range(PLANE // 2):
+        a = mqs[2 * m]
+        b = mqs[2 * m + 1] if 2 * m + 1 < PLANE - 1 else mq[...]
+        low = jnp.where(low_half, a, pltpu.roll(b, G, 1))
+        high = jnp.where(low_half, pltpu.roll(a, G, 1), b)
+        low = jnp.where(sub < 12, low, jnp.where(sub == 12, masses[m], 0.0))
+        high = jnp.where(sub < 12, high, 0.0)
+        for i, part in enumerate(split3(jnp.concatenate([low, high], axis=0))):
+            split[pl.ds(i * 32, 32), pl.ds(m * 128, 128)] = part.astype(BF16)
+    blocks = lax.dot_general(hot[...], split[...], NT_DIMS, preferred_element_type=F32)
+    blocks = blocks + pltpu.roll(blocks, 96, 1) + pltpu.roll(blocks, 64, 1)
+    lane = iota((8, 128), 1)
+    first = iota((8, 128), 0) == 0
+    shared = jnp.where(
+        first & (lane >= 32) & (lane < 48),
+        pltpu.roll(sums, 32, 1)[0:1],
+        jnp.where(first & (lane >= 48) & (lane < 64), pltpu.roll(sums, 48, 1)[1:2], 0.0),
+    )
+    for i in range(ZLINE):
+        tile[i] = jnp.where(lane < 32, blocks[i * 8 : (i + 1) * 8], shared)
     start_line(1)
-    wait_all(mzs.at[1], zr.at[1])
-    row = mz[1] + total(mzs[1, i] for i in range(ZLINE - 1))
-    below = row[2:3, :]
+    wait_all(tiles, zr.at[1])
+    mine = tile[me_z] + total(tiles[i] for i in range(ZLINE - 1))
+    row = jnp.concatenate(
+        [pltpu.roll(mine, 96, 1)[0:1], pltpu.roll(mine, 80, 1)[0:1]], axis=0
+    )
 
     inverse = [1.0 / s for s in guess]
 
@@ -646,7 +684,7 @@
                 out[i + 1] = e
         return out
 
-    _, answer, left = sweeps(entries(row[0:2, :], ITERS + 1), ITERS, newton)
+    _, answer, left = sweeps(entries(row, ITERS + 1), ITERS, newton)
 
     def combine(coefficients, f):
         return total(
@@ -658,20 +696,19 @@
         for f, out in enumerate((state_out, adjoint_out)):
             out[own[a]] = solved[f][a * LAYER : (a + 1) * LAYER, :DOF].reshape(NY, NZ, DOF)
     applied = {i: (1.0 - c if i == 0 else -c) for i, c in left.items()}
-    applied = [combine(applied, f) for f in range(2)]
-    bracket = jnp.sum(solved[1] * applied[0] + solved[0] * applied[1], axis=1, keepdims=True)
-    weighted = density * (-1.5 * bracket / density)
-    mp[2, 0:1, :] = as_row(weighted)
-    start_plane(2)
-    wait_all(mps.at[2], pr.at[2])
-    mz[2, 0:1, :] = by_block(2, 0)
-    start_line(2)
-    wait_all(mzs.at[2], zr.at[2])
-    above = mz[2, 0:1, :] + total(mzs[2, i, 0:1, :] for i in range(ZLINE - 1))
+    lane = iota((1, 128), 1)
+    weights = jnp.zeros((1, 128), F32)
+    for (i, j), spot in spots.items():
+        terms = []
+        if i < ITERS:
+            terms.append(answer[i][1:2] * applied[j][0:1])
+        if j < ITERS:
+            terms.append(answer[j][0:1] * applied[i][1:2])
+        weights = jnp.where(lane == spot, total(terms), weights)
+    above = -1.5 * jnp.sum(mine * weights, axis=1, keepdims=True)
+    below = mine[:, 12:13]
     ratio = jnp.where(below > 0.0, above / below, 0.0)
-    mine = iota((8, 128), 1) == iota((8, 128), 0) + 8 * me_z
-    col = jnp.sum(jnp.where(mine, ratio, 0.0), axis=1, keepdims=True)
-    coarse_out[...] = jnp.sum(jnp.where(eye8, col, 0.0), axis=0, keepdims=True)
+    coarse_out[...] = jnp.sum(jnp.where(eye8, ratio, 0.0), axis=0, keepdims=True)
 
     for k in range(ITERS):
         for_halos(k, range(6), [c for c, _ in sends], lambda copy: copy.wait_send())
@@ -686,9 +723,8 @@
         for m in range(2, 4):
             far_copy(m).wait_send()
 
-    for e in range(3):
-        wait_all(mps.at[e], ps.at[e])
-        wait_all(mzs.at[e], zs.at[e])
+    for buffer, sem in ((mps, ps.at[0]), (mqs, ps.at[1]), (mzs, zs.at[0]), (tiles, zs.at[1])):
+        wait_all(buffer, sem)
 
 
 def local(body_load, probe_load, density, link_types, off_blocks, self_blocks, block_owner):
@@ -716,18 +752,23 @@
             pltpu.VMEM((ALL, LANES), F32),
             pltpu.VMEM((128, PLANE * G), BF16),
             pltpu.VMEM((32, 128), F32),
-            pltpu.VMEM((3, 4, 128), F32),
-            pltpu.VMEM((3, PLANE - 1, 4, 128), F32),
-            pltpu.VMEM((3, 4, 128), F32),
-            pltpu.VMEM((3, ZLINE - 1, 4, 128), F32),
+            pltpu.VMEM((4, 128), F32),
+            pltpu.VMEM((PLANE - 1, 4, 128), F32),
+            pltpu.VMEM((4, 128), F32),
+            pltpu.VMEM((ZLINE - 1, 4, 128), F32),
+            pltpu.VMEM((16, 128), F32),
+            pltpu.VMEM((PLANE - 1, 16, 128), F32),
+            pltpu.VMEM((128, PLANE * G), BF16),
+            pltpu.VMEM((ZLINE, 8, 128), F32),
+            pltpu.VMEM((ZLINE - 1, 8, 128), F32),
             pltpu.SemaphoreType.DMA((ITERS, 6)),
             pltpu.SemaphoreType.DMA((ITERS, 6)),
             pltpu.SemaphoreType.DMA((4,)),
             pltpu.SemaphoreType.DMA((4,)),
-            pltpu.SemaphoreType.DMA((3,)),
-            pltpu.SemaphoreType.DMA((3,)),
-            pltpu.SemaphoreType.DMA((3,)),
-            pltpu.SemaphoreType.DMA((3,)),
+            pltpu.SemaphoreType.DMA((2,)),
+            pltpu.SemaphoreType.DMA((2,)),
+            pltpu.SemaphoreType.DMA((2,)),
+            pltpu.SemaphoreType.DMA((2,)),
         ],
         compiler_params=pltpu.CompilerParams(
             collective_id=0, has_side_effects=True, vmem_limit_bytes=60 << 20

time: 80.7 us -> 69.9 us (0.87)
  Pallas kernels: 77.2 us -> 65.6 us
    pallas_call x1, Pallas kernels: 77.2 us -> 65.6 us  [local(): pl.pallas_call(kernel, out_shape=(jax.ShapeDtypeStruct(body_load.shape, F...]
where the time goes in v4:
time: 69.9 us; the launch traced here: 68.9 us
  Pallas kernels  65.6 us (94%)
  local copies, waits for them, and re-layouts  2.65 us (4%)
    pallas_call x1, Pallas kernels, local(): pl.pallas_call(kernel, out_shape=(jax.ShapeDtypeStruct(body_load.shape, F...  65.6 us
    unnamed x7, local copies, waits for them, and re-layouts  2.65 us

profile of v4, /device:TPU:1, one launch (start us, length us, event | category | flops | bytes accessed | tf_op | source)
XLA Modules:
  0.0 68.9 jit_solution(16047258212518975971)
XLA Ops:
  0.6 65.6 %sweeps.1 = (f32[2,4,8,192]{3,2,1,0:T(8,128)}, f32[2,4,8,192]{3,2,1,0:T(8,128)}, f32[1,8]{1,0:T(1,128)}) custom-call(f32[2,4,8,192]{3,2,1,0:T(8,128)} %body.1, f32[2,4,8,192]{3,2,1,0:T(8,128)} %probe.1, f32[2,4,8]{2,1,0:T(4,128)} %dens.1, s32[2,7,4,8]{3,2,1,0:T(4,128)} %bitcast.2, bf16[4,192,192]{2,1,0:T(8,128)(2,1)} %offb.1, bf16[4,192,192]{2,1,0:T(8,128)(2,1)} %selfb.1, ...), custom_call_target="tpu_custom_call" | custom-call | tf_op jit(solution)/shard_map/sweeps/pallas_call | solution.py:732
  66.2 0.0 copy-start
  66.3 1.5 %copy.13 = f32[2,4,8,192]{3,2,1,0:T(8,128)} copy(f32[2,4,8,192]{3,2,1,0:T(8,128)} %get-tuple-element.12) | data formatting | bytes 98304
  67.8 0.0 copy-done
  67.8 0.0 copy-start.1
  67.8 0.6 copy.14
  68.4 0.0 copy-done.1
  68.4 0.5 copy.15
Async XLA Ops:
  66.2 1.5 %copy-start = (f32[2,4,8,192]{3,2,1,0:T(8,128)S(1)}, f32[2,4,8,192]{3,2,1,0:T(8,128)}, u32[]{:S(2)}) copy-start(f32[2,4,8,192]{3,2,1,0:T(8,128)} %get-tuple-element.13) | copy-start | bytes 147460
  67.8 0.6 copy-start.1

commit v5 on v4

--- a/solution.py
+++ b/solution.py
@@ -77,7 +77,7 @@
 
 
 def kernel(body, probe, dens, links, offb, selfb, owner, state_out, adjoint_out, coarse_out,
-           x_one, x_two, faces_one, faces_two, vg, pick, table, v, su, sc, rp, hot, rr, mp, mps, mz, mzs, mq, mqs, split, tile, tiles,
+           x_one, x_two, faces_one, faces_two, vg, pick, table, v, su, sc, rp, hot, rr, mp, mps, mz, mzs, mq, mqs, me, mes, split, tile, tiles,
            hs, hr, fs, fr, ps, pr, zs, zr):
     gx, gy, gz = lax.axis_index("gx"), lax.axis_index("gy"), lax.axis_index("gz")
     zh, yc = gx // CY, gx % CY
@@ -438,8 +438,10 @@
         def one(i, _):
             if e == 0:
                 src, dst = mp, mps.at[PLANE - 2 - i]
+            elif e == 1:
+                src, dst = mq, mqs.at[PLANE - 2 - i]
             else:
-                src, dst = mq, mqs.at[PLANE - 2 - i]
+                src, dst = me, mes.at[PLANE - 2 - i]
             pltpu.make_async_remote_copy(
                 src_ref=src, dst_ref=dst, send_sem=ps.at[e], recv_sem=pr.at[e],
                 device_id=plane_peer(i), device_id_type=MESH,
@@ -583,10 +585,13 @@
         vg[f] = parts[f][G:].astype(F32) * beyond
 
     spots = {}
-    for i in range(ITERS + 1):
-        for j in range(ITERS + 1):
-            if i + j < 2 * ITERS:
-                spots[i, j] = len(spots) % 12 + 16 * (len(spots) // 12)
+    for i in range(ITERS):
+        for j in range(ITERS):
+            n = len(spots)
+            spots[i, j] = n % 8 + 16 * (n // 8)
+    for i in range(ITERS):
+        spots[i, ITERS] = 8 + i
+        spots[ITERS, i] = 24 + i
     lane = iota((G, 128), 1)
     columns = [jnp.zeros((G, 128), F32)]
 
@@ -594,6 +599,12 @@
         part = v[i, pl.ds(G, G), :] * rp[pl.ds(0, G), :] * v[j, pl.ds(0, G), :]
         col = jnp.sum(part, axis=1, keepdims=True)
         columns[0] = jnp.where(lane == spots[i, j], col, columns[0])
+
+    def turned(at):
+        rows = jnp.transpose(jnp.concatenate([columns[0], jnp.zeros((G, 128), F32)], axis=0))
+        return jnp.where(
+            low_half, rows[at : at + 8], pltpu.roll(rows[at + 16 : at + 24], G, 1)
+        )
 
     guess = None
     for k in range(ITERS):
@@ -634,19 +645,26 @@
             products(k + 1, i)
         if 0 < k + 1 < ITERS:
             products(k + 1, k + 1)
+        if k == ITERS - 2:
+            me[...] = turned(0)
+            start_plane(2)
 
     rows = gram_rows()
-    turned = jnp.transpose(jnp.concatenate([columns[0], jnp.zeros((G, 128), F32)], axis=0))
-    mq[...] = jnp.where(low_half, turned[0:16], pltpu.roll(turned[16:32], G, 1))
-    mq[12:13, :] = rows[0]
-    mq[13:14, :] = rows[1]
+    mq[...] = turned(8)
+    mq[4:5, :] = rows[0]
+    mq[5:6, :] = rows[1]
     start_plane(1)
+    wait_all(mes, pr.at[2])
     wait_all(mqs, pr.at[1])
-    sums = mq[12:14, :] + total(mqs[i, 12:14, :] for i in range(PLANE - 1))
+    sums = mq[4:6, :] + total(mqs[i, 4:6, :] for i in range(PLANE - 1))
+
+    def message(i):
+        parts = [mes[i], mqs[i]] if i < PLANE - 1 else [me[...], mq[...]]
+        return jnp.concatenate(parts, axis=0)
+
     sub = iota((16, 128), 0)
     for m in range(PLANE // 2):
-        a = mqs[2 * m]
-        b = mqs[2 * m + 1] if 2 * m + 1 < PLANE - 1 else mq[...]
+        a, b = message(2 * m), message(2 * m + 1)
         low = jnp.where(low_half, a, pltpu.roll(b, G, 1))
         high = jnp.where(low_half, pltpu.roll(a, G, 1), b)
         low = jnp.where(sub < 12, low, jnp.where(sub == 12, masses[m], 0.0))
@@ -663,10 +681,12 @@
         jnp.where(first & (lane >= 48) & (lane < 64), pltpu.roll(sums, 48, 1)[1:2], 0.0),
     )
     for i in range(ZLINE):
-        tile[i] = jnp.where(lane < 32, blocks[i * 8 : (i + 1) * 8], shared)
+        full = jnp.where(lane < 32, blocks[i * 8 : (i + 1) * 8], shared)
+        tile[i] = jnp.where(low_half, full[0:4], pltpu.roll(full, G, 1)[4:8])
     start_line(1)
     wait_all(tiles, zr.at[1])
     mine = tile[me_z] + total(tiles[i] for i in range(ZLINE - 1))
+    mine = jnp.concatenate([mine, pltpu.roll(mine, G, 1)], axis=0)
     row = jnp.concatenate(
         [pltpu.roll(mine, 96, 1)[0:1], pltpu.roll(mine, 80, 1)[0:1]], axis=0
     )
@@ -723,8 +743,20 @@
         for m in range(2, 4):
             far_copy(m).wait_send()
 
-    for buffer, sem in ((mps, ps.at[0]), (mqs, ps.at[1]), (mzs, zs.at[0]), (tiles, zs.at[1])):
+    for buffer, sem in (
+        (mps, ps.at[0]),
+        (mqs, ps.at[1]),
+        (mes, ps.at[2]),
+        (mzs, zs.at[0]),
+        (tiles, zs.at[1]),
+    ):
         wait_all(buffer, sem)
+
+
+def deliver(state, adjoint, coarse, state_out, adjoint_out, coarse_out):
+    state_out[...] = state[...]
+    adjoint_out[...] = adjoint[...]
+    coarse_out[...] = coarse[...]
 
 
 def local(body_load, probe_load, density, link_types, off_blocks, self_blocks, block_owner):
@@ -756,17 +788,19 @@
             pltpu.VMEM((PLANE - 1, 4, 128), F32),
             pltpu.VMEM((4, 128), F32),
             pltpu.VMEM((ZLINE - 1, 4, 128), F32),
-            pltpu.VMEM((16, 128), F32),
-            pltpu.VMEM((PLANE - 1, 16, 128), F32),
+            pltpu.VMEM((8, 128), F32),
+            pltpu.VMEM((PLANE - 1, 8, 128), F32),
+            pltpu.VMEM((8, 128), F32),
+            pltpu.VMEM((PLANE - 1, 8, 128), F32),
             pltpu.VMEM((128, PLANE * G), BF16),
-            pltpu.VMEM((ZLINE, 8, 128), F32),
-            pltpu.VMEM((ZLINE - 1, 8, 128), F32),
+            pltpu.VMEM((ZLINE, 4, 128), F32),
+            pltpu.VMEM((ZLINE - 1, 4, 128), F32),
             pltpu.SemaphoreType.DMA((ITERS, 6)),
             pltpu.SemaphoreType.DMA((ITERS, 6)),
             pltpu.SemaphoreType.DMA((4,)),
             pltpu.SemaphoreType.DMA((4,)),
-            pltpu.SemaphoreType.DMA((2,)),
-            pltpu.SemaphoreType.DMA((2,)),
+            pltpu.SemaphoreType.DMA((3,)),
+            pltpu.SemaphoreType.DMA((3,)),
             pltpu.SemaphoreType.DMA((2,)),
             pltpu.SemaphoreType.DMA((2,)),
         ],
@@ -783,6 +817,17 @@
         self_blocks,
         block_owner,
     )
+    state, adjoint, coarse = pl.pallas_call(
+        deliver,
+        out_shape=(
+            jax.ShapeDtypeStruct(body_load.shape, F32),
+            jax.ShapeDtypeStruct(body_load.shape, F32),
+            jax.ShapeDtypeStruct((1, GPB), F32),
+        ),
+        in_specs=[vmem] * 3,
+        out_specs=(vmem,) * 3,
+        name="deliver",
+    )(state, adjoint, coarse)
     return state, adjoint, coarse.reshape(GPB)
 
 

time: 69.9 us -> 68 us (0.973); the launches traced: 68.9 us -> 67.8 us
  local copies, waits for them, and re-layouts: 2.65 us -> 0 us
  Pallas kernels: 65.6 us -> 67.2 us
    unnamed x7 -> x0, local copies, waits for them, and re-layouts: 2.65 us -> none
    pallas_call x0 -> x1, Pallas kernels: none -> 1.53 us  [local(): pl.pallas_call(deliver, out_shape=(jax.ShapeDtypeStruct(body_load.shape,...]
where the time goes in v5:
time: 68 us; the launch traced here: 67.8 us
  Pallas kernels  67.2 us (99%)
    pallas_call x1, Pallas kernels, local(): pl.pallas_call(kernel, out_shape=(jax.ShapeDtypeStruct(body_load.shape, F...  65.7 us
    pallas_call x1, Pallas kernels, local(): pl.pallas_call(deliver, out_shape=(jax.ShapeDtypeStruct(body_load.shape,...  1.53 us

profile of v5, /device:TPU:1, one launch (start us, length us, event | category | flops | bytes accessed | tf_op | source)
XLA Modules:
  0.0 67.8 jit_solution(9457176558482725946)
XLA Ops:
  0.6 65.7 %sweeps.1 = (f32[2,4,8,192]{3,2,1,0:T(8,128)}, f32[2,4,8,192]{3,2,1,0:T(8,128)}, f32[1,8]{1,0:T(1,128)}) custom-call(f32[2,4,8,192]{3,2,1,0:T(8,128)} %body.1, f32[2,4,8,192]{3,2,1,0:T(8,128)} %probe.1, f32[2,4,8]{2,1,0:T(4,128)} %dens.1, s32[2,7,4,8]{3,2,1,0:T(4,128)} %bitcast.2, bf16[4,192,192]{2,1,0:T(8,128)(2,1)} %offb.1, bf16[4,192,192]{2,1,0:T(8,128)(2,1)} %selfb.1, ...), custom_call_target="tpu_custom_call" | custom-call | tf_op jit(solution)/shard_map/sweeps/pallas_call | solution.py:764
  66.3 1.5 %deliver.1 = (f32[2,4,8,192]{3,2,1,0:T(8,128)}, f32[2,4,8,192]{3,2,1,0:T(8,128)}, f32[1,8]{1,0:T(1,128)}) custom-call(f32[2,4,8,192]{3,2,1,0:T(8,128)} %get-tuple-element.9.state, f32[2,4,8,192]{3,2,1,0:T(8,128)} %get-tuple-element.10.adjoint, f32[1,8]{1,0:T(1,128)} %get-tuple-element.11.coarse), custom_call_target="tpu_custom_call" | custom-call | tf_op jit(solution)/shard_map/deliver/pallas_call | solution.py:820

commit v6 on v5

--- a/solution.py
+++ b/solution.py
@@ -753,20 +753,14 @@
         wait_all(buffer, sem)
 
 
-def deliver(state, adjoint, coarse, state_out, adjoint_out, coarse_out):
-    state_out[...] = state[...]
-    adjoint_out[...] = adjoint[...]
-    coarse_out[...] = coarse[...]
-
-
 def local(body_load, probe_load, density, link_types, off_blocks, self_blocks, block_owner):
     vmem = pl.BlockSpec(memory_space=pltpu.VMEM)
     state, adjoint, coarse = pl.pallas_call(
         kernel,
         out_shape=(
-            jax.ShapeDtypeStruct(body_load.shape, F32),
-            jax.ShapeDtypeStruct(body_load.shape, F32),
-            jax.ShapeDtypeStruct((1, GPB), F32),
+            pltpu.VMEM(body_load.shape, F32),
+            pltpu.VMEM(body_load.shape, F32),
+            pltpu.VMEM((1, GPB), F32),
         ),
         in_specs=[vmem] * 7,
         out_specs=(vmem,) * 3,
@@ -817,17 +811,6 @@
         self_blocks,
         block_owner,
     )
-    state, adjoint, coarse = pl.pallas_call(
-        deliver,
-        out_shape=(
-            jax.ShapeDtypeStruct(body_load.shape, F32),
-            jax.ShapeDtypeStruct(body_load.shape, F32),
-            jax.ShapeDtypeStruct((1, GPB), F32),
-        ),
-        in_specs=[vmem] * 3,
-        out_specs=(vmem,) * 3,
-        name="deliver",
-    )(state, adjoint, coarse)
     return state, adjoint, coarse.reshape(GPB)
 
 

time: 68 us -> 67.6 us (level)
  Pallas kernels: 67.2 us -> 65 us
  local copies, waits for them, and re-layouts: 0 us -> 1.77 us
    pallas_call x2 -> x1, Pallas kernels: 67.2 us -> 65 us  [local(): pl.pallas_call(kernel, out_shape=(pltpu.VMEM(body_load.shape, F32), pltpu...]
    unnamed x0 -> x3, local copies, waits for them, and re-layouts: none -> 1.77 us
where the time goes in v6:
time: 67.6 us; the launch traced here: 67.4 us
  Pallas kernels  65 us (96%)
  local copies, waits for them, and re-layouts  1.77 us (3%)
    pallas_call x1, Pallas kernels, local(): pl.pallas_call(kernel, out_shape=(pltpu.VMEM(body_load.shape, F32), pltpu...  65 us
    unnamed x3, local copies, waits for them, and re-layouts  1.77 us

profile of v6, /device:TPU:1, one launch (start us, length us, event | category | flops | bytes accessed | tf_op | source)
XLA Modules:
  0.0 67.4 jit_solution(17041681298004212967)
XLA Ops:
  0.6 65.0 %sweeps.1 = (f32[2,4,8,192]{3,2,1,0:T(8,128)S(1)}, f32[2,4,8,192]{3,2,1,0:T(8,128)S(1)}, f32[1,8]{1,0:T(1,128)S(1)}) custom-call(f32[2,4,8,192]{3,2,1,0:T(8,128)} %body.1, f32[2,4,8,192]{3,2,1,0:T(8,128)} %probe.1, f32[2,4,8]{2,1,0:T(4,128)} %dens.1, s32[2,7,4,8]{3,2,1,0:T(4,128)} %bitcast.3, bf16[4,192,192]{2,1,0:T(8,128)(2,1)} %offb.1, ...), custom_call_target="tpu_custom_call" | custom-call | tf_op jit(solution)/shard_map/sweeps/pallas_call | solution.py:758
  65.7 0.6 copy.13
  66.3 0.5 copy.15
  66.8 0.6 copy.14
